TPU v7x, 128 devices: a whole 4x4x4 slice. The times are simulated.
128 devices in a mesh: rows: 16 (over y, z), cols: 8 (over x, core).
Axes of the slice: x: 4, y: 4, z: 4, core: 2. Of those that a mesh axis runs over, the one named last changes fastest.
Arguments:
- queries: bfloat16 [32768, 768], P('rows')
- candidates: bfloat16 [262144, 768], P(('rows', 'cols'))
- requests: int32 [2048, 1], P(('rows', 'cols')), may hold values from 0 to 7, as said below
- pairs: int32 [16384, 2], P(('rows', 'cols')), may hold values from 0 to 15, as said below
- counts: int32 [128], P(('rows', 'cols')), may hold values from 1 to 128, as said below
Outputs:
- scores: bfloat16 [16384, 256, 256], P(('rows', 'cols'))
- row_weights: float32 [32768], P('rows')
Inputs may be any that keep to these rules, and one draw needn't show every extreme that they name: `requests`: each row lists 1 distinct local block indices. `pairs`: column 0 is below 8; column 1 is a fetch slot below 16. `counts`: slots at or beyond a device's count are padding.
All inputs are finite; a program needn't handle non-finite values.
Results may differ from a plain program's by a relative error of at most 0.0004.
Values may be sent and summed in bfloat16 or wider, within the bound.
No kernel may reach another device: no remote copies, remote signals or barrier semaphores. Data moves between devices by JAX's collectives and lax.ppermute only.
A program may use at most 128 MiB of HBM per device.

v0:
```python
import math

import jax
import jax.numpy as jnp
from jax import lax
from jax.sharding import PartitionSpec as P

BLK = 256


def inverse_norm(values):
    wide = values.astype(jnp.float32)
    return lax.rsqrt(jnp.mean(wide * wide, axis=-1) + 1e-06)


def selector(indices, width, dtype):
    return (indices[:, None] == jnp.arange(width, dtype=jnp.int32)[None, :]).astype(dtype)


def per_device(queries, candidates, requests, pairs, counts):
    row_count = lax.axis_size("rows")
    feature_dim = queries.shape[1]
    fetch_count = requests.shape[1]
    pair_count = pairs.shape[0]
    query_blocks = queries.reshape(-1, BLK, feature_dim)
    cand_blocks = candidates.reshape(-1, BLK, feature_dim)
    block_total = query_blocks.shape[0]
    local_total = cand_blocks.shape[0]
    fetched_total = row_count * fetch_count
    scale = 1.0 / math.sqrt(feature_dim)
    wanted = lax.all_to_all(requests, "rows", split_axis=0, concat_axis=0, tiled=True)
    pick_local = selector(wanted.reshape(-1), local_total, jnp.bfloat16)
    outgoing = jnp.einsum(
        "fb,bid->fid", pick_local, cand_blocks, preferred_element_type=jnp.float32
    ).astype(jnp.bfloat16)
    outgoing = outgoing.reshape(row_count, fetch_count, BLK, feature_dim)
    inv_q = inverse_norm(query_blocks)
    query_ids = pairs[:, 0]
    slot_ids = pairs[:, 1]
    live_mask = (jnp.arange(pair_count, dtype=jnp.int32) < counts[0]).astype(jnp.float32)
    arrived = lax.all_to_all(outgoing, "rows", split_axis=0, concat_axis=0, tiled=True)
    fetched = arrived.reshape(fetched_total, BLK, feature_dim)
    inv_c = inverse_norm(fetched)

    def group_dots(group_q, group_c):
        pick_q = selector(group_q, block_total, jnp.bfloat16)
        pick_c = selector(group_c, fetched_total, jnp.bfloat16)
        q_rows = jnp.einsum(
            "pq,qid->pid", pick_q, query_blocks, preferred_element_type=jnp.float32
        ).astype(jnp.bfloat16)
        c_rows = jnp.einsum(
            "pc,cid->pid", pick_c, fetched, preferred_element_type=jnp.float32
        ).astype(jnp.bfloat16)
        return jnp.einsum("pid,pjd->pij", q_rows, c_rows, preferred_element_type=jnp.float32)

    def tile_group(first_pair):
        group_q = lax.dynamic_slice_in_dim(query_ids, first_pair, 8, 0)
        group_c = lax.dynamic_slice_in_dim(slot_ids, first_pair, 8, 0)
        group_live = lax.dynamic_slice_in_dim(live_mask, first_pair, 8, 0)
        dots = group_dots(group_q, group_c)
        scale_q = jnp.einsum(
            "pq,qi->pi",
            selector(group_q, block_total, jnp.float32),
            inv_q,
            precision=lax.Precision.HIGHEST,
        )
        scale_c = jnp.einsum(
            "pc,cj->pj",
            selector(group_c, fetched_total, jnp.float32),
            inv_c,
            precision=lax.Precision.HIGHEST,
        )
        zvals = dots * scale_q[:, :, None] * scale_c[:, None, :] * scale
        positive = jnp.maximum(zvals - 1.0, 0.0) * group_live[:, None, None]
        return (positive.astype(jnp.bfloat16), jnp.sum(positive, axis=-1))

    firsts = jnp.arange(0, pair_count, 8, dtype=jnp.int32)
    tiles, sums_part = lax.map(tile_group, firsts)
    scores = tiles.reshape(pair_count, BLK, BLK)
    row_terms = sums_part.reshape(pair_count, BLK)
    one_hot = selector(query_ids, block_total, jnp.float32)
    local_sums = jnp.einsum("pq,pb->qb", one_hot, row_terms, precision=lax.Precision.HIGHEST)
    totals = lax.psum(local_sums.reshape(-1), "cols")
    row_weights = totals / BLK
    return (scores, row_weights)


def solution(mesh):
    in_specs = (
        P("rows", None),
        P(("rows", "cols"), None),
        P(("rows", "cols"), None),
        P(("rows", "cols"), None),
        P(("rows", "cols")),
    )
    out_specs = (P(("rows", "cols"), None, None), P("rows"))
    return jax.shard_map(
        per_device, mesh=mesh, in_specs=in_specs, out_specs=out_specs, check_vma=False
    )
```

profile of v0, /device:TPU:80, one launch (start us, length us, event | category | flops | bytes accessed | tf_op | source)
XLA Modules:
  0.0 408.6 jit_solution(5663498743059220290)
XLA Ops:
  1.5 10.8 %all_to_all.14 = s32[16,1,1]{2,1,0:T(1,128)S(1)} all-to-all(s32[16,1,1]{2,1,0:T(1,128)S(1)} %copy.40), channel_id=1, replica_groups=mesh['rows'=16,'cols'=8] {'rows'}, dimensions={0} | all-to-all | bytes 128 | tf_op jit(solution)/shard_map/all_to_all | solution.py:31
  15.2 4.8 %copy.42 = bf16[16,1,256,768]{3,2,1,0:T(8,128)(2,1)} copy(bf16[16,1,256,768]{3,0,2,1:T(8,128)(2,1)S(1)} %convert_bitcast_fusion.1) | data formatting | bytes 12582912 | tf_op jit(solution)/shard_map/reshape | solution.py:36
  20.0 8.6 %all-to-all-start.1 = ((bf16[16,1,256,768]{3,2,1,0:T(8,128)(2,1)}), bf16[16,1,256,768]{3,2,1,0:T(8,128)(2,1)}, u32[]{:S(2)}, u32[]{:S(2)}) async-start(bf16[16,1,256,768]{3,2,1,0:T(8,128)(2,1)} %copy.42), calls=%async_computation.1 | async-start | bytes 12582912 | tf_op jit(solution)/shard_map/all_to_all | solution.py:41
  31.8 5.3 %copy.45 = bf16[8,256,768]{2,0,1:T(8,128)(2,1)} copy(bf16[8,256,768]{2,1,0:T(8,128)(2,1)} %bitcast.55) | data formatting | bytes 6291456 | tf_op jit(solution)/shard_map/while | solution.py:78
  37.1 88.1 %all-to-all-done.1 = bf16[16,1,256,768]{3,2,1,0:T(8,128)(2,1)} async-done(((bf16[16,1,256,768]{3,2,1,0:T(8,128)(2,1)}), bf16[16,1,256,768]{3,2,1,0:T(8,128)(2,1)}, u32[]{:S(2)}, u32[]{:S(2)}) %all-to-all-start.1) | async-done | bytes 6291488 | tf_op jit(solution)/shard_map/all_to_all | solution.py:41
  125.2 4.1 multiply_reduce_fusion
  129.3 9.0 %copy.46 = bf16[16,256,768]{2,0,1:T(8,128)(2,1)} copy(bf16[16,256,768]{2,1,0:T(8,128)(2,1)} %bitcast.12) | data formatting | bytes 12582912 | tf_op jit(solution)/shard_map/while | solution.py:78
  138.3 256.8 %while.14 = (s32[]{:T(128)}, bf16[16,8,256,256]{3,2,1,0:T(8,128)(2,1)}, f32[16,8,256]{2,1,0:T(8,128)S(1)}, s32[16]{0:T(128)S(1)}, s32[128]{0:T(128)S(1)}, /*inde...) while((s32[]{:T(128)}, ...), condition=%wide.region_4.5_spmd, body=%wide.region_2.4_spmd.sunk | while | flops 888732032 | bytes 39928392 | solution.py:78
  141.2 4.0 convolution_convert_fusion.4
  146.2 3.5 fusion.53
  157.2 4.0 convolution_convert_fusion.4
  173.3 4.0 convolution_convert_fusion.4
  189.3 4.0 convolution_convert_fusion.4
  194.4 3.5 fusion.53
  205.4 4.0 convolution_convert_fusion.4
  210.4 3.5 fusion.53
  221.4 4.0 convolution_convert_fusion.4
  226.5 3.5 fusion.53
  237.5 4.0 convolution_convert_fusion.4
  253.5 4.0 convolution_convert_fusion.4
  258.6 3.5 fusion.53
  269.6 4.0 convolution_convert_fusion.4
  274.6 3.5 fusion.53
  285.6 4.0 convolution_convert_fusion.4
  301.7 4.0 convolution_convert_fusion.4
  317.7 4.0 convolution_convert_fusion.4
  333.8 4.0 convolution_convert_fusion.4
  349.8 4.0 convolution_convert_fusion.4
  365.9 4.0 convolution_convert_fusion.4
  381.9 4.0 convolution_convert_fusion.4
  387.0 3.5 fusion.53
  395.3 12.7 %psum.7 = f32[2048]{0:T(1024)S(1)} all-reduce(f32[2048]{0:T(1024)S(1)} %bitcast.56), channel_id=1, replica_groups=mesh['rows'=16,'cols'=8] {'cols'}, use_global_device_ids=true, to_apply=%region_5.6 | all-reduce | flops 2048 | bytes 16384 | tf_op jit(solution)/shard_map/psum | solution.py:83
  (220 shorter events, 147.1 us)
Async XLA Ops:
  0.6 12.1 %copy-start = (bf16[2048,768]{1,0:T(8,128)(2,1)S(1)}, bf16[2048,768]{1,0:T(8,128)(2,1)}, u32[]{:S(2)}) copy-start(bf16[2048,768]{1,0:T(8,128)(2,1)} %param.8) | copy-start | bytes 9437188
  20.0 105.2 %all-to-all-start.1 = ((bf16[16,1,256,768]{3,2,1,0:T(8,128)(2,1)}), bf16[16,1,256,768]{3,2,1,0:T(8,128)(2,1)}, u32[]{:S(2)}, u32[]{:S(2)}) async-start(bf16[16,1,256,768]{3,2,1,0:T(8,128)(2,1)} %copy.42), calls=%async_computation.1 | async-start | bytes 12582912 | tf_op jit(solution)/shard_map/all_to_all | solution.py:41
  31.8 5.3 %copy-start.2 = (s32[128,2]{0,1:T(2,128)S(1)}, s32[128,2]{0,1:T(2,128)}, u32[]{:S(2)}) copy-start(s32[128,2]{0,1:T(2,128)} %param.10) | copy-start | bytes 3076
  141.2 4.0 copy-start.1
  157.2 4.0 copy-start.1
  173.3 4.0 copy-start.1
  189.3 4.0 copy-start.1
  205.4 4.0 copy-start.1
  221.4 4.0 copy-start.1
  237.5 4.0 copy-start.1
  253.5 4.0 copy-start.1
  269.6 4.0 copy-start.1
  285.6 4.0 copy-start.1
  301.7 4.0 copy-start.1
  317.7 4.0 copy-start.1
  333.8 4.0 copy-start.1
  349.8 4.0 copy-start.1
  365.9 4.0 copy-start.1
  381.9 4.0 copy-start.1
where the time goes:
time: 410 us; the launch traced here: 409 us
  matrix products  146 us (36%)
  local copies, waits for them, and re-layouts  106 us (26%)
  waiting for transfers between devices  88.1 us (21%)
  loops' own time  28 us (7%)
  blocking collectives  23.5 us (6%)
  starting transfers between devices  8.58 us (2%)
  other arithmetic  7.66 us (2%)
    all_to_all x1, waiting for transfers between devices, per_device(): lax.all_to_all(outgoing, 'rows', split_axis=0, concat_axis=0, tiled=True)  88.1 us
    dynamic_update_slice x48, local copies, waits for them, and re-layouts, per_device(): tiles, sums_part = lax.map(tile_group, firsts)  72.6 us
    dot_general x16, matrix products, group_dots(): jnp.einsum('pc,cid->pid', pick_c, fetched, preferred_element_type=jnp.flo...  64 us
    dot_general x16, matrix products, group_dots(): jnp.einsum('pid,pjd->pij', q_rows, c_rows, preferred_element_type=jnp.flo...  56.8 us
    another operation x1, loops' own time, per_device(): tiles, sums_part = lax.map(tile_group, firsts)  28 us
    dot_general x16, matrix products, group_dots(): jnp.einsum('pq,qid->pid', pick_q, query_blocks, preferred_element_type=jn...  16.4 us
    while x2, local copies, waits for them, and re-layouts, per_device(): tiles, sums_part = lax.map(tile_group, firsts)  14.3 us
    psum x1, blocking collectives, per_device(): totals = lax.psum(local_sums.reshape(-1), 'cols')  12.7 us
  transfers between devices with their start and end apart: 1, of which 1 were waited for; matrix products, arithmetic and copies ran while one was open for 2% of the time, Pallas kernels for 0%

commit v1 on v0

v1 whole, which is shorter than its diff:
```python
import functools
import math

import jax
import jax.numpy as jnp
from jax import lax
from jax.experimental import pallas as pl
from jax.experimental.pallas import tpu as pltpu
from jax.sharding import PartitionSpec as P

BLK = 256
LANES = 128
RING = 4
ZRING = 16
WINDOW = 5
HEAD = 3
ORDER = (
    (1, 1), (3, 3), (1, 3), (3, 1), (2, 0), (0, 2), (2, 1), (0, 3),
    (2, 3), (0, 1), (1, 2), (3, 0), (3, 2), (1, 0), (2, 2),
)
CALLS = ((0, 4), (4, 8), (8, 12), (12, 15), (15, 16))


def inverse_norm(values):
    wide = values.astype(jnp.float32)
    return lax.rsqrt(jnp.mean(wide * wide, axis=-1) + 1e-06)


def pair_kernel(first, n_src, zero_fill, feature_dim, meta, *refs):
    q_hbm, iq_hbm = refs[:2]
    srcs = refs[2 : 2 + n_src]
    out, sums, q, iq, cbuf, ic, acc, ring, zero, qsem, iqsem, csem, osem, zsem = refs[-14:]
    n_pairs = out.shape[0]
    ranks_row = 3
    lo = meta[ranks_row, first]
    hi = meta[ranks_row, first + n_src]
    copies = []
    for i in range(n_src):
        copies.append(pltpu.make_async_copy(srcs[i], cbuf.at[i], csem.at[i]))
    q_copy = pltpu.make_async_copy(q_hbm, q, qsem)
    iq_copy = pltpu.make_async_copy(iq_hbm, iq, iqsem)
    copies[0].start()
    q_copy.start()
    iq_copy.start()
    for copy in copies[1:]:
        copy.start()
    acc[...] = jnp.zeros_like(acc)
    if zero_fill:
        zero[...] = jnp.zeros_like(zero)
        dead = meta[ranks_row, 16]

        def zero_copy(j):
            return pltpu.make_async_copy(
                zero, out.at[meta[0, j]], zsem.at[lax.rem(j - dead, ZRING)]
            )

        @pl.loop(dead, n_pairs)
        def _(j):
            @pl.when(j >= dead + ZRING)
            def _():
                zero_copy(j - ZRING).wait()

            zero_copy(j).start()

    ones = jnp.ones((8, feature_dim), jnp.bfloat16)
    dims = (((1,), (1,)), ((), ()))
    scale = 1.0 / math.sqrt(feature_dim)
    for i in range(n_src):
        copies[i].wait()
        wide = cbuf[i].astype(jnp.float32)
        square = wide * wide
        high = square.astype(jnp.bfloat16)
        low = (square - high.astype(jnp.float32)).astype(jnp.bfloat16)
        total = lax.dot_general(ones, high, dims, preferred_element_type=jnp.float32)
        total += lax.dot_general(ones, low, dims, preferred_element_type=jnp.float32)
        ic[i] = lax.rsqrt(total * (1.0 / feature_dim) + 1e-06) * scale
    q_copy.wait()
    iq_copy.wait()

    def score(j, slot, weight):
        qb = meta[1, j]
        c = meta[2, j] - first
        rows = pl.ds(pl.multiple_of(qb * BLK, BLK), BLK)
        dots = lax.dot_general(q[rows, :], cbuf[c], dims, preferred_element_type=jnp.float32)
        inv_q = iq[rows, :]
        inv_c = ic[c, 0:1, :]
        total = None
        for h in range(BLK // LANES):
            cols = slice(h * LANES, (h + 1) * LANES)
            pos = jnp.maximum(dots[:, cols] * inv_q * inv_c[:, cols] - 1.0, 0.0)
            ring[slot, :, cols] = pos.astype(jnp.bfloat16)
            total = pos if total is None else total + pos
        if weight is not None:
            total = total * weight
        acc[qb] += total

    def out_copy(j, slot):
        return pltpu.make_async_copy(ring.at[slot], out.at[meta[0, j]], osem.at[slot])

    half = RING // 2
    steps = (hi - lo + 1) // 2

    @pl.loop(0, steps)
    def _(i):
        slot = lax.rem(i, half) * 2
        a = lo + 2 * i
        b = jnp.minimum(a + 1, hi - 1)

        @pl.when(i >= half)
        def _():
            out_copy(a - RING, slot).wait()
            out_copy(a - RING + 1, slot + 1).wait()

        score(a, slot, None)
        score(b, slot + 1, (a + 1 < hi).astype(jnp.float32))
        out_copy(a, slot).start()

        @pl.when(a + 1 < hi)
        def _():
            out_copy(b, slot + 1).start()

    @pl.loop(jnp.maximum(lo, lo + 2 * (steps - half)), hi)
    def _(j):
        out_copy(j, lax.rem(j - lo, RING)).wait()

    if zero_fill:

        @pl.loop(jnp.maximum(dead, n_pairs - ZRING), n_pairs)
        def _(j):
            zero_copy(j).wait()

    sums[...] = jnp.sum(acc[...], axis=-1)


def take_kernel(codes, wanted, to, candidates, *refs):
    outs, sem = refs[:-1], refs[-1]
    copies = []
    for i, code in enumerate(codes):
        start = pl.multiple_of(wanted[to[code]] * BLK, BLK)
        copies.append(
            pltpu.make_async_copy(candidates.at[pl.ds(start, BLK)], outs[i], sem.at[i])
        )
    for copy in copies:
        copy.start()
    for copy in copies:
        copy.wait()


def take_blocks(offsets, wanted, to, candidates):
    side = math.isqrt(to.shape[0])
    smem = pl.BlockSpec(memory_space=pltpu.SMEM)
    hbm = pl.BlockSpec(memory_space=pl.ANY)
    codes = tuple(dy * side + dz for dy, dz in offsets)
    return list(
        pl.pallas_call(
            functools.partial(take_kernel, codes),
            out_shape=(
                jax.ShapeDtypeStruct((BLK, candidates.shape[1]), candidates.dtype),
            )
            * len(codes),
            in_specs=[smem, smem, pl.BlockSpec(memory_space=pltpu.HBM)],
            out_specs=(hbm,) * len(codes),
            scratch_shapes=[pltpu.SemaphoreType.DMA((len(codes),))],
            compiler_params=pltpu.CompilerParams(vmem_limit_bytes=1 << 20),
            name="take_%d" % len(codes),
        )(wanted, to, candidates)
    )


def score_pairs(first, sources, zero_fill, n_pairs, meta, queries, inv_q, *out):
    n_src = len(sources)
    feature_dim = queries.shape[1]
    q_rows = queries.shape[0]
    blocks = q_rows // BLK
    pairs_here = max(n_pairs * n_src // 16, 1)
    hbm = pl.BlockSpec(memory_space=pl.ANY)
    return pl.pallas_call(
        functools.partial(pair_kernel, first, n_src, zero_fill, feature_dim),
        out_shape=(
            jax.ShapeDtypeStruct((n_pairs, BLK, BLK), jnp.bfloat16),
            jax.ShapeDtypeStruct((blocks, BLK), jnp.float32),
        ),
        in_specs=[pl.BlockSpec(memory_space=pltpu.SMEM)] + [hbm] * (n_src + 2 + len(out)),
        out_specs=(hbm, pl.BlockSpec(memory_space=pltpu.VMEM)),
        scratch_shapes=[
            pltpu.VMEM((q_rows, feature_dim), jnp.bfloat16),
            pltpu.VMEM((q_rows, LANES), jnp.float32),
            pltpu.VMEM((n_src, BLK, feature_dim), jnp.bfloat16),
            pltpu.VMEM((n_src, 8, BLK), jnp.float32),
            pltpu.VMEM((blocks, BLK, LANES), jnp.float32),
            pltpu.VMEM((RING, BLK, BLK), jnp.bfloat16),
            pltpu.VMEM((BLK, BLK), jnp.bfloat16),
            pltpu.SemaphoreType.DMA,
            pltpu.SemaphoreType.DMA,
            pltpu.SemaphoreType.DMA((n_src,)),
            pltpu.SemaphoreType.DMA((RING,)),
            pltpu.SemaphoreType.DMA((ZRING,)),
        ],
        input_output_aliases={3 + n_src: 0} if out else {},
        cost_estimate=pl.CostEstimate(
            flops=2 * pairs_here * BLK * BLK * feature_dim,
            bytes_accessed=pairs_here * BLK * BLK * 2,
            transcendentals=0,
        ),
        compiler_params=pltpu.CompilerParams(vmem_limit_bytes=24 << 20),
        name="pairs_%d" % first,
    )(meta, queries, inv_q, *sources, *out)


def per_device(queries, candidates, requests, pairs, counts):
    row_count = lax.axis_size("rows")
    side = math.isqrt(row_count)
    col_count = lax.axis_size("cols")
    feature_dim = queries.shape[1]
    pair_count = pairs.shape[0]
    me = lax.axis_index("rows")
    my_y, my_z = me // side, me % side
    wanted = lax.all_to_all(requests, "rows", split_axis=0, concat_axis=0, tiled=True)[:, 0]

    offsets = ((0, 0),) + ORDER
    rank_of = [0] * row_count
    for rank, (dy, dz) in enumerate(offsets):
        rank_of[dy * side + dz] = rank
    slots = pairs[:, 1]
    away = ((my_y - slots // side) % side) * side + (my_z - slots % side) % side
    ids = jnp.arange(pair_count, dtype=jnp.int32)
    rank = jnp.zeros_like(slots)
    for code, value in enumerate(rank_of):
        rank = rank + jnp.where(away == code, value, 0)
    rank = jnp.where(ids < counts[0], rank, row_count)
    before = (rank[None, :] < rank[:, None]) | (
        (rank[None, :] == rank[:, None]) & (ids[None, :] < ids[:, None])
    )
    place = jnp.sum(before.astype(jnp.int32), axis=1)
    at = place[None, :] == ids[:, None]
    sorted_ids = jnp.sum(jnp.where(at, ids[None, :], 0), axis=1)
    sorted_q = jnp.sum(jnp.where(at, pairs[:, 0][None, :], 0), axis=1)
    sorted_rank = jnp.sum(jnp.where(at, rank[None, :], 0), axis=1)
    starts = jnp.sum((rank[None, :] < ids[:, None]).astype(jnp.int32), axis=1)
    meta = jnp.stack([sorted_ids, sorted_q, sorted_rank, starts])

    inv_q = jnp.broadcast_to(inverse_norm(queries)[:, None], (queries.shape[0], LANES))
    codes = jnp.arange(row_count, dtype=jnp.int32)
    to = ((my_y + codes // side) % side) * side + (my_z + codes % side) % side
    sends = take_blocks(ORDER[:HEAD], wanted, to, candidates)
    sends += take_blocks(ORDER[HEAD:] + ((0, 0),), wanted, to, candidates)
    arrived = [sends.pop()]
    out, local = None, None
    for k, (dy, dz) in enumerate(ORDER):
        send = sends[k]
        if k >= WINDOW:
            send, arrived[k - WINDOW + 1] = lax.optimization_barrier(
                (send, arrived[k - WINDOW + 1])
            )
        perm = [
            (y * side + z, ((y + dy) % side) * side + (z + dz) % side)
            for y in range(side)
            for z in range(side)
        ]
        arrived.append(lax.ppermute(send, "rows", perm))
    for call, (lo, hi) in enumerate(CALLS):
        out, sums = score_pairs(
            lo, arrived[lo:hi], call == 0, pair_count, meta, queries, inv_q,
            *(() if out is None else (out,)),
        )
        local = sums if local is None else local + sums
    totals = local.reshape(-1)
    step = 1
    while step < col_count:
        totals = totals + lax.ppermute(totals, "cols", [(i, i ^ step) for i in range(col_count)])
        step *= 2
    return out, totals * (1.0 / BLK)


def solution(mesh):
    in_specs = (
        P("rows", None),
        P(("rows", "cols"), None),
        P(("rows", "cols"), None),
        P(("rows", "cols"), None),
        P(("rows", "cols")),
    )
    out_specs = (P(("rows", "cols"), None, None), P("rows"))
    return jax.shard_map(
        per_device, mesh=mesh, in_specs=in_specs, out_specs=out_specs, check_vma=False
    )
```

time: 410 us -> 155 us (0.38)
  the two profiles are of different devices: /device:TPU:80 before, /device:TPU:68 now
where the time goes in v1:
time: 155 us
  starting transfers between devices  59.4 us (38%)
  Pallas kernels  45.1 us (29%)
  waiting for transfers between devices  35.6 us (23%)
  local copies, waits for them, and re-layouts  7.48 us (5%)
  other arithmetic  5.42 us (3%)
    pallas_call x5, Pallas kernels, score_pairs(): pl.pallas_call(functools.partial(pair_kernel, first, n_src, zero_fill, fe...  40.4 us
    ppermute x15, starting transfers between devices, per_device(): arrived.append(lax.ppermute(send, 'rows', perm))  32.9 us
    ppermute x15, waiting for transfers between devices, per_device(): arrived.append(lax.ppermute(send, 'rows', perm))  24.6 us
    ppermute x3, starting transfers between devices, per_device(): lax.ppermute(totals, 'cols', [(i, i ^ step) for i in range(col_count)])  18.9 us
    ppermute x3, waiting for transfers between devices, per_device(): lax.ppermute(totals, 'cols', [(i, i ^ step) for i in range(col_count)])  7.94 us
    all_to_all x1, starting transfers between devices, per_device(): lax.all_to_all(requests, 'rows', split_axis=0, concat_axis=0, tiled=True)  7.61 us
    unnamed x9, local copies, waits for them, and re-layouts  5.68 us
    pallas_call x2, Pallas kernels, take_blocks(): pl.pallas_call(functools.partial(take_kernel, codes), out_shape=(jax.Shap...  4.71 us
  transfers between devices with their start and end apart: 19, of which 7 were waited for; matrix products, arithmetic and copies ran while one was open for 3% of the time, Pallas kernels for 25%

profile of v1, /device:TPU:68, one launch (start us, length us, event | category | flops | bytes accessed | tf_op | source)
XLA Modules:
  0.0 154.6 jit_solution(2074808952626579510)
XLA Ops:
  0.6 1.5 copy.13
  2.1 7.6 %all-to-all-start = ((s32[16,1,1]{2,1,0:T(1,128)}), s32[16,1,1]{2,1,0:T(1,128)S(1)}, u32[]{:S(2)}, u32[]{:S(2)}) async-start(s32[16,1,1]{2,1,0:T(1,128)} %copy.13), calls=%async_computation | async-start | bytes 16384 | tf_op jit(solution)/shard_map/all_to_all | solution.py:218
  11.9 3.1 %all-to-all-done = s32[16,1,1]{2,1,0:T(1,128)S(1)} async-done(((s32[16,1,1]{2,1,0:T(1,128)}), s32[16,1,1]{2,1,0:T(1,128)S(1)}, u32[]{:S(2)}, u32[]{:S(2)}) %all-to-all-start) | async-done | bytes 96 | tf_op jit(solution)/shard_map/all_to_all | solution.py:218
  15.4 1.9 %copy-done.2 = bf16[2048,768]{1,0:T(8,128)(2,1)S(1)} copy-done((bf16[2048,768]{1,0:T(8,128)(2,1)S(1)}, bf16[2048,768]{1,0:T(8,128)(2,1)}, u32[]{:S(2)}) %copy-start.2) | copy-done | bytes 3145752
  17.3 1.1 take_3.1
  18.4 1.5 collective-permute-start.12
  19.9 2.6 %multiply_reduce_fusion = f32[2048]{0:T(1024)S(1)} fusion(bf16[2048,768]{1,0:T(8,128)(2,1)} %refs_0_.9), kind=kLoop, calls=%fused_computation | loop fusion | flops 4716544 | bytes 3153920 | tf_op jit(solution)/shard_map/reduce_sum | solution.py:26
  22.5 1.9 %copy-done.3 = bf16[2048,768]{1,0:T(8,128)(2,1)S(1)} copy-done((bf16[2048,768]{1,0:T(8,128)(2,1)S(1)}, bf16[2048,768]{1,0:T(8,128)(2,1)}, u32[]{:S(2)}) %copy-start.3) | copy-done | bytes 3145752
  24.4 3.6 %take_13.1 = (bf16[256,768]{1,0:T(8,128)(2,1)S(1)}, bf16[256,768]{1,0:T(8,128)(2,1)S(1)}, bf16[256,768]{1,0:T(8,128)(2,1)S(1)}, bf16[256,768]{1,0:T(8,128)(2,1)S...) custom-call(s32[16]{0:T(128)S(1)} %reduce.wanted, ...), custom_call_target="tpu_custom_call" | custom-call | tf_op jit(solution)/shard_map/take_13/pallas_call | solution.py:155
  28.0 2.8 %collective-permute-start.3 = (bf16[256,768]{1,0:T(8,128)(2,1)S(1)}, bf16[256,768]{1,0:T(8,128)(2,1)S(1)}, u32[]{:S(2)}, u32[]{:S(2)}) collective-permute-start(bf16[256,768]{1,0:T(8,128)(2,1)S(1)} %get-tuple-element.55), channel_id=1, source_target_pairs={{0,120},{8,96},{16,104},{24,112},{32,24},{40,0},{48,8},{56,16},{64... | collective-permute-start | bytes 1179656 | tf_op jit(solution)/shard_map/ppermute | solution.py:260
  31.0 2.1 %collective-permute-start = (bf16[256,768]{1,0:T(8,128)(2,1)S(1)}, bf16[256,768]{1,0:T(8,128)(2,1)S(1)}, u32[]{:S(2)}, u32[]{:S(2)}) collective-permute-start(bf16[256,768]{1,0:T(8,128)(2,1)S(1)} %get-tuple-element.50), channel_id=1, source_target_pairs={{0,64},{8,72},{16,80},{24,88},{32,96},{40,104},{48,112},{56,120},{... | collective-permute-start | bytes 1179656 | tf_op jit(solution)/shard_map/ppermute | solution.py:260
  33.0 1.9 %collective-permute-start.9 = (bf16[256,768]{1,0:T(8,128)(2,1)S(1)}, bf16[256,768]{1,0:T(8,128)(2,1)S(1)}, u32[]{:S(2)}, u32[]{:S(2)}) collective-permute-start(bf16[256,768]{1,0:T(8,128)(2,1)S(1)} %get-tuple-element.65), channel_id=1, source_target_pairs={{0,104},{8,112},{16,120},{24,96},{32,8},{40,16},{48,24},{56,0},{64... | collective-permute-start | bytes 1179656 | tf_op jit(solution)/shard_map/ppermute | solution.py:260
  35.1 3.6 %collective-permute-start.13 = (bf16[256,768]{1,0:T(8,128)(2,1)S(1)}, bf16[256,768]{1,0:T(8,128)(2,1)S(1)}, u32[]{:S(2)}, u32[]{:S(2)}) collective-permute-start(bf16[256,768]{1,0:T(8,128)(2,1)S(1)} %get-tuple-element.74), channel_id=1, source_target_pairs={{0,16},{8,24},{16,0},{24,8},{32,48},{40,56},{48,32},{56,40},{64,80... | collective-permute-start | bytes 1179656 | tf_op jit(solution)/shard_map/ppermute | solution.py:260
  38.8 10.5 %collective-permute-done.3.refs_4_ = bf16[256,768]{1,0:T(8,128)(2,1)S(1)} collective-permute-done((bf16[256,768]{1,0:T(8,128)(2,1)S(1)}, bf16[256,768]{1,0:T(8,128)(2,1)S(1)}, u32[]{:S(2)}, u32[]{:S(2)}) %collective-permute-start.3) | collective-permute-done | bytes 393248 | tf_op jit(solution)/shard_map/ppermute | solution.py:260
  49.3 1.9 %collective-permute-start.7 = (bf16[256,768]{1,0:T(8,128)(2,1)S(1)}, bf16[256,768]{1,0:T(8,128)(2,1)S(1)}, u32[]{:S(2)}, u32[]{:S(2)}) collective-permute-start(bf16[256,768]{1,0:T(8,128)(2,1)S(1)} %get-tuple-element.61), channel_id=1, source_target_pairs={{0,24},{8,0},{16,8},{24,16},{32,56},{40,32},{48,40},{56,48},{64,88... | collective-permute-start | bytes 1179656 | tf_op jit(solution)/shard_map/ppermute | solution.py:260
  51.2 1.1 collective-permute-start.4
  52.3 4.4 %collective-permute-done.refs_3_ = bf16[256,768]{1,0:T(8,128)(2,1)S(1)} collective-permute-done((bf16[256,768]{1,0:T(8,128)(2,1)S(1)}, bf16[256,768]{1,0:T(8,128)(2,1)S(1)}, u32[]{:S(2)}, u32[]{:S(2)}) %collective-permute-start) | collective-permute-done | bytes 393248 | tf_op jit(solution)/shard_map/ppermute | solution.py:260
  56.7 4.0 %collective-permute-start.1 = (bf16[256,768]{1,0:T(8,128)(2,1)S(1)}, bf16[256,768]{1,0:T(8,128)(2,1)S(1)}, u32[]{:S(2)}, u32[]{:S(2)}) collective-permute-start(bf16[256,768]{1,0:T(8,128)(2,1)S(1)} %get-tuple-element.51), channel_id=1, source_target_pairs={{0,8},{8,16},{16,24},{24,0},{32,40},{40,48},{48,56},{56,32},{64,72... | collective-permute-start | bytes 1179656 | tf_op jit(solution)/shard_map/ppermute | solution.py:260
  60.7 9.7 %collective-permute-done.9.refs_2_ = bf16[256,768]{1,0:T(8,128)(2,1)S(1)} collective-permute-done((bf16[256,768]{1,0:T(8,128)(2,1)S(1)}, bf16[256,768]{1,0:T(8,128)(2,1)S(1)}, u32[]{:S(2)}, u32[]{:S(2)}) %collective-permute-start.9) | collective-permute-done | bytes 393248 | tf_op jit(solution)/shard_map/ppermute | solution.py:260
  71.3 6.5 %collective-permute-start.14 = (bf16[256,768]{1,0:T(8,128)(2,1)S(1)}, bf16[256,768]{1,0:T(8,128)(2,1)S(1)}, u32[]{:S(2)}, u32[]{:S(2)}) collective-permute-start(bf16[256,768]{1,0:T(8,128)(2,1)S(1)} %get-tuple-element.75), channel_id=1, source_target_pairs={{0,48},{8,56},{16,32},{24,40},{32,80},{40,88},{48,64},{56,72},{64,... | collective-permute-start | bytes 1179656 | tf_op jit(solution)/shard_map/ppermute | solution.py:260
  78.1 1.9 %copy-done = bf16[2048,768]{1,0:T(8,128)(2,1)S(1)} copy-done((bf16[2048,768]{1,0:T(8,128)(2,1)S(1)}, bf16[2048,768]{1,0:T(8,128)(2,1)}, u32[]{:S(2)}) %copy-start) | copy-done | bytes 3145752
  80.0 13.1 %pairs_0.1 = (bf16[128,256,256]{2,1,0:T(8,128)(2,1)}, f32[8,256]{1,0:T(8,128)S(1)}) custom-call(s32[4,128]{1,0:T(4,128)S(1)} %pad_add_fusion.meta, bf16[2048,768]{1,0:T(8,128)(2,1)S(1)} %copy-done, f32[2048,128]{1,0:T(8,128)S(1)} %broadcast_in_dim.121.refs_1_, bf16[256,768]{1,0:T(8,128)(2,1)S(1)} %get-tuple-element.80.refs_2_, ...), custom_call_target="tpu_custom_call" | custom-call | flops 3221225472 | bytes 4194304 | tf_op jit(solution)/shard_map/pairs_0/pallas_call | solution.py:177
  93.2 2.2 %collective-permute-start.5 = (bf16[256,768]{1,0:T(8,128)(2,1)S(1)}, bf16[256,768]{1,0:T(8,128)(2,1)S(1)}, u32[]{:S(2)}, u32[]{:S(2)}) collective-permute-start(bf16[256,768]{1,0:T(8,128)(2,1)S(1)} %get-tuple-element.57), channel_id=1, source_target_pairs={{0,96},{8,104},{16,112},{24,120},{32,0},{40,8},{48,16},{56,24},{64... | collective-permute-start | bytes 1179656 | tf_op jit(solution)/shard_map/ppermute | solution.py:260
  95.4 4.3 %collective-permute-start.2 = (bf16[256,768]{1,0:T(8,128)(2,1)S(1)}, bf16[256,768]{1,0:T(8,128)(2,1)S(1)}, u32[]{:S(2)}, u32[]{:S(2)}) collective-permute-start(bf16[256,768]{1,0:T(8,128)(2,1)S(1)} %get-tuple-element.52), channel_id=1, source_target_pairs={{0,80},{8,88},{16,64},{24,72},{32,112},{40,120},{48,96},{56,104},{... | collective-permute-start | bytes 1179656 | tf_op jit(solution)/shard_map/ppermute | solution.py:260
  99.7 8.2 %pairs_4.1 = (bf16[128,256,256]{2,1,0:T(8,128)(2,1)}, f32[8,256]{1,0:T(8,128)S(1)}) custom-call(s32[4,128]{1,0:T(4,128)S(1)} %pad_add_fusion.meta, bf16[2048,768]{1,0:T(8,128)(2,1)S(1)} %copy-done.1, f32[2048,128]{1,0:T(8,128)S(1)} %broadcast_in_dim.121.refs_1_, ...), custom_call_target="tpu_custom_call", output_to_operand_aliasing={{0}: (7, {})} | custom-call | flops 3221225472 | bytes 4194304 | tf_op jit(solution)/shard_map/pairs_4/pallas_call | solution.py:177
  108.0 8.2 %pairs_8.1 = (bf16[128,256,256]{2,1,0:T(8,128)(2,1)}, f32[8,256]{1,0:T(8,128)S(1)}) custom-call(s32[4,128]{1,0:T(4,128)S(1)} %pad_add_fusion.meta, bf16[2048,768]{1,0:T(8,128)(2,1)S(1)} %copy-done.1, f32[2048,128]{1,0:T(8,128)S(1)} %broadcast_in_dim.121.refs_1_, ...), custom_call_target="tpu_custom_call", output_to_operand_aliasing={{0}: (7, {})} | custom-call | flops 3221225472 | bytes 4194304 | tf_op jit(solution)/shard_map/pairs_8/pallas_call | solution.py:177
  116.2 6.2 %pairs_12.1 = (bf16[128,256,256]{2,1,0:T(8,128)(2,1)}, f32[8,256]{1,0:T(8,128)S(1)}) custom-call(s32[4,128]{1,0:T(4,128)S(1)} %pad_add_fusion.meta, bf16[2048,768]{1,0:T(8,128)(2,1)S(1)} %copy-done.1, f32[2048,128]{1,0:T(8,128)S(1)} %broadcast_in_dim.121.refs_1_, ...), custom_call_target="tpu_custom_call", output_to_operand_aliasing={{0}: (6, {})} | custom-call | flops 2415919104 | bytes 3145728 | tf_op jit(solution)/shard_map/pairs_12/pallas_call | solution.py:177
  122.4 4.7 %pairs_15.1 = (bf16[128,256,256]{2,1,0:T(8,128)(2,1)}, f32[8,256]{1,0:T(8,128)S(1)}) custom-call(s32[4,128]{1,0:T(4,128)S(1)} %pad_add_fusion.meta, bf16[2048,768]{1,0:T(8,128)(2,1)S(1)} %copy-done.1, f32[2048,128]{1,0:T(8,128)S(1)} %broadcast_in_dim.121.refs_1_, ...), custom_call_target="tpu_custom_call", output_to_operand_aliasing={{0}: (4, {})} | custom-call | flops 805306368 | bytes 1048576 | tf_op jit(solution)/shard_map/pairs_15/pallas_call | solution.py:177
  127.2 1.2 collective-permute-done.15
  128.4 18.8 %collective-permute-start.16 = (f32[2048]{0:T(1024)S(1)}, f32[2048]{0:T(1024)S(1)}, u32[]{:S(2)}, u32[]{:S(2)}) collective-permute-start(f32[2048]{0:T(1024)S(1)} %add.309), channel_id=1, source_target_pairs={{0,2},{1,3},{2,0},{3,1},{4,6},{5,7},{6,4},{7,5},{8,10},{9,11},{10,... | collective-permute-start | bytes 24584 | tf_op jit(solution)/shard_map/ppermute | solution.py:270
  147.2 1.6 %collective-permute-done.16 = f32[2048]{0:T(1024)S(1)} collective-permute-done((f32[2048]{0:T(1024)S(1)}, f32[2048]{0:T(1024)S(1)}, u32[]{:S(2)}, u32[]{:S(2)}) %collective-permute-start.16) | collective-permute-done | bytes 8224 | tf_op jit(solution)/shard_map/ppermute | solution.py:270
  148.8 5.2 %collective-permute-done.17 = f32[2048]{0:T(1024)S(1)} collective-permute-done((f32[2048]{0:T(1024)S(1)}, f32[2048]{0:T(1024)S(1)}, u32[]{:S(2)}, u32[]{:S(2)}) %collective-permute-start.17) | collective-permute-done | bytes 8224 | tf_op jit(solution)/shard_map/ppermute | solution.py:270
  (37 shorter events, 4.5 us)
Async XLA Ops:
  0.6 99.1 %copy-start.1 = (bf16[2048,768]{1,0:T(8,128)(2,1)S(1)}, bf16[2048,768]{1,0:T(8,128)(2,1)}, u32[]{:S(2)}) copy-start(bf16[2048,768]{1,0:T(8,128)(2,1)} %refs_0_.9) | copy-start | bytes 9437188
  2.1 12.9 %all-to-all-start = ((s32[16,1,1]{2,1,0:T(1,128)}), s32[16,1,1]{2,1,0:T(1,128)S(1)}, u32[]{:S(2)}, u32[]{:S(2)}) async-start(s32[16,1,1]{2,1,0:T(1,128)} %copy.13), calls=%async_computation | async-start | bytes 16384 | tf_op jit(solution)/shard_map/all_to_all | solution.py:218
  15.4 1.9 %copy-start.2 = (bf16[2048,768]{1,0:T(8,128)(2,1)S(1)}, bf16[2048,768]{1,0:T(8,128)(2,1)}, u32[]{:S(2)}) copy-start(bf16[2048,768]{1,0:T(8,128)(2,1)} %candidates.3) | copy-start | bytes 9437188
  18.4 16.6 %collective-permute-start.12 = (bf16[256,768]{1,0:T(8,128)(2,1)S(1)}, bf16[256,768]{1,0:T(8,128)(2,1)S(1)}, u32[]{:S(2)}, u32[]{:S(2)}) collective-permute-start(bf16[256,768]{1,0:T(8,128)(2,1)S(1)} %get-tuple-element.73), channel_id=1, source_target_pairs={{0,40},{8,48},{16,56},{24,32},{32,72},{40,80},{48,88},{56,64},{64,... | collective-permute-start | bytes 1179656 | tf_op jit(solution)/shard_map/ppermute | solution.py:260
  22.5 1.9 %copy-start.3 = (bf16[2048,768]{1,0:T(8,128)(2,1)S(1)}, bf16[2048,768]{1,0:T(8,128)(2,1)}, u32[]{:S(2)}) copy-start(bf16[2048,768]{1,0:T(8,128)(2,1)} %candidates.3) | copy-start | bytes 9437188
  28.0 21.3 %collective-permute-start.3 = (bf16[256,768]{1,0:T(8,128)(2,1)S(1)}, bf16[256,768]{1,0:T(8,128)(2,1)S(1)}, u32[]{:S(2)}, u32[]{:S(2)}) collective-permute-start(bf16[256,768]{1,0:T(8,128)(2,1)S(1)} %get-tuple-element.55), channel_id=1, source_target_pairs={{0,120},{8,96},{16,104},{24,112},{32,24},{40,0},{48,8},{56,16},{64... | collective-permute-start | bytes 1179656 | tf_op jit(solution)/shard_map/ppermute | solution.py:260
  30.7 18.6 %collective-permute-start.6 = (bf16[256,768]{1,0:T(8,128)(2,1)S(1)}, bf16[256,768]{1,0:T(8,128)(2,1)S(1)}, u32[]{:S(2)}, u32[]{:S(2)}) collective-permute-start(bf16[256,768]{1,0:T(8,128)(2,1)S(1)} %get-tuple-element.60), channel_id=1, source_target_pairs={{0,56},{8,32},{16,40},{24,48},{32,88},{40,64},{48,72},{56,80},{64,... | collective-permute-start | bytes 1179656 | tf_op jit(solution)/shard_map/ppermute | solution.py:260
  31.0 25.7 %collective-permute-start = (bf16[256,768]{1,0:T(8,128)(2,1)S(1)}, bf16[256,768]{1,0:T(8,128)(2,1)S(1)}, u32[]{:S(2)}, u32[]{:S(2)}) collective-permute-start(bf16[256,768]{1,0:T(8,128)(2,1)S(1)} %get-tuple-element.50), channel_id=1, source_target_pairs={{0,64},{8,72},{16,80},{24,88},{32,96},{40,104},{48,112},{56,120},{... | collective-permute-start | bytes 1179656 | tf_op jit(solution)/shard_map/ppermute | solution.py:260
  33.0 37.4 %collective-permute-start.9 = (bf16[256,768]{1,0:T(8,128)(2,1)S(1)}, bf16[256,768]{1,0:T(8,128)(2,1)S(1)}, u32[]{:S(2)}, u32[]{:S(2)}) collective-permute-start(bf16[256,768]{1,0:T(8,128)(2,1)S(1)} %get-tuple-element.65), channel_id=1, source_target_pairs={{0,104},{8,112},{16,120},{24,96},{32,8},{40,16},{48,24},{56,0},{64... | collective-permute-start | bytes 1179656 | tf_op jit(solution)/shard_map/ppermute | solution.py:260
  35.1 36.2 %collective-permute-start.13 = (bf16[256,768]{1,0:T(8,128)(2,1)S(1)}, bf16[256,768]{1,0:T(8,128)(2,1)S(1)}, u32[]{:S(2)}, u32[]{:S(2)}) collective-permute-start(bf16[256,768]{1,0:T(8,128)(2,1)S(1)} %get-tuple-element.74), channel_id=1, source_target_pairs={{0,16},{8,24},{16,0},{24,8},{32,48},{40,56},{48,32},{56,40},{64,80... | collective-permute-start | bytes 1179656 | tf_op jit(solution)/shard_map/ppermute | solution.py:260
  49.3 43.8 %collective-permute-start.7 = (bf16[256,768]{1,0:T(8,128)(2,1)S(1)}, bf16[256,768]{1,0:T(8,128)(2,1)S(1)}, u32[]{:S(2)}, u32[]{:S(2)}) collective-permute-start(bf16[256,768]{1,0:T(8,128)(2,1)S(1)} %get-tuple-element.61), channel_id=1, source_target_pairs={{0,24},{8,0},{16,8},{24,16},{32,56},{40,32},{48,40},{56,48},{64,88... | collective-permute-start | bytes 1179656 | tf_op jit(solution)/shard_map/ppermute | solution.py:260
  51.2 42.0 %collective-permute-start.4 = (bf16[256,768]{1,0:T(8,128)(2,1)S(1)}, bf16[256,768]{1,0:T(8,128)(2,1)S(1)}, u32[]{:S(2)}, u32[]{:S(2)}) collective-permute-start(bf16[256,768]{1,0:T(8,128)(2,1)S(1)} %get-tuple-element.56), channel_id=1, source_target_pairs={{0,72},{8,80},{16,88},{24,64},{32,104},{40,112},{48,120},{56,96},{... | collective-permute-start | bytes 1179656 | tf_op jit(solution)/shard_map/ppermute | solution.py:260
  56.7 38.7 %collective-permute-start.1 = (bf16[256,768]{1,0:T(8,128)(2,1)S(1)}, bf16[256,768]{1,0:T(8,128)(2,1)S(1)}, u32[]{:S(2)}, u32[]{:S(2)}) collective-permute-start(bf16[256,768]{1,0:T(8,128)(2,1)S(1)} %get-tuple-element.51), channel_id=1, source_target_pairs={{0,8},{8,16},{16,24},{24,0},{32,40},{40,48},{48,56},{56,32},{64,72... | collective-permute-start | bytes 1179656 | tf_op jit(solution)/shard_map/ppermute | solution.py:260
  70.4 29.3 %collective-permute-start.10 = (bf16[256,768]{1,0:T(8,128)(2,1)S(1)}, bf16[256,768]{1,0:T(8,128)(2,1)S(1)}, u32[]{:S(2)}, u32[]{:S(2)}) collective-permute-start(bf16[256,768]{1,0:T(8,128)(2,1)S(1)} %get-tuple-element.66), channel_id=1, source_target_pairs={{0,88},{8,64},{16,72},{24,80},{32,120},{40,96},{48,104},{56,112},{... | collective-permute-start | bytes 1179656 | tf_op jit(solution)/shard_map/ppermute | solution.py:260
  71.3 36.7 %collective-permute-start.14 = (bf16[256,768]{1,0:T(8,128)(2,1)S(1)}, bf16[256,768]{1,0:T(8,128)(2,1)S(1)}, u32[]{:S(2)}, u32[]{:S(2)}) collective-permute-start(bf16[256,768]{1,0:T(8,128)(2,1)S(1)} %get-tuple-element.75), channel_id=1, source_target_pairs={{0,48},{8,56},{16,32},{24,40},{32,80},{40,88},{48,64},{56,72},{64,... | collective-permute-start | bytes 1179656 | tf_op jit(solution)/shard_map/ppermute | solution.py:260
  78.1 1.9 %copy-start = (bf16[2048,768]{1,0:T(8,128)(2,1)S(1)}, bf16[2048,768]{1,0:T(8,128)(2,1)}, u32[]{:S(2)}) copy-start(bf16[2048,768]{1,0:T(8,128)(2,1)} %refs_0_.9) | copy-start | bytes 9437188
  93.1 23.1 %collective-permute-start.8 = (bf16[256,768]{1,0:T(8,128)(2,1)S(1)}, bf16[256,768]{1,0:T(8,128)(2,1)S(1)}, u32[]{:S(2)}, u32[]{:S(2)}) collective-permute-start(bf16[256,768]{1,0:T(8,128)(2,1)S(1)} %get-tuple-element.62), channel_id=1, source_target_pairs={{0,112},{8,120},{16,96},{24,104},{32,16},{40,24},{48,0},{56,8},{64... | collective-permute-start | bytes 1179656 | tf_op jit(solution)/shard_map/ppermute | solution.py:260
  93.2 23.0 %collective-permute-start.5 = (bf16[256,768]{1,0:T(8,128)(2,1)S(1)}, bf16[256,768]{1,0:T(8,128)(2,1)S(1)}, u32[]{:S(2)}, u32[]{:S(2)}) collective-permute-start(bf16[256,768]{1,0:T(8,128)(2,1)S(1)} %get-tuple-element.57), channel_id=1, source_target_pairs={{0,96},{8,104},{16,112},{24,120},{32,0},{40,8},{48,16},{56,24},{64... | collective-permute-start | bytes 1179656 | tf_op jit(solution)/shard_map/ppermute | solution.py:260
  95.4 27.0 %collective-permute-start.2 = (bf16[256,768]{1,0:T(8,128)(2,1)S(1)}, bf16[256,768]{1,0:T(8,128)(2,1)S(1)}, u32[]{:S(2)}, u32[]{:S(2)}) collective-permute-start(bf16[256,768]{1,0:T(8,128)(2,1)S(1)} %get-tuple-element.52), channel_id=1, source_target_pairs={{0,80},{8,88},{16,64},{24,72},{32,112},{40,120},{48,96},{56,104},{... | collective-permute-start | bytes 1179656 | tf_op jit(solution)/shard_map/ppermute | solution.py:260
  99.7 16.5 %collective-permute-start.11 = (bf16[256,768]{1,0:T(8,128)(2,1)S(1)}, bf16[256,768]{1,0:T(8,128)(2,1)S(1)}, u32[]{:S(2)}, u32[]{:S(2)}) collective-permute-start(bf16[256,768]{1,0:T(8,128)(2,1)S(1)} %get-tuple-element.67), channel_id=1, source_target_pairs={{0,32},{8,40},{16,48},{24,56},{32,64},{40,72},{48,80},{56,88},{64,... | collective-permute-start | bytes 1179656 | tf_op jit(solution)/shard_map/ppermute | solution.py:260
  127.1 1.3 collective-permute-start.15
  128.4 20.4 %collective-permute-start.16 = (f32[2048]{0:T(1024)S(1)}, f32[2048]{0:T(1024)S(1)}, u32[]{:S(2)}, u32[]{:S(2)}) collective-permute-start(f32[2048]{0:T(1024)S(1)} %add.309), channel_id=1, source_target_pairs={{0,2},{1,3},{2,0},{3,1},{4,6},{5,7},{6,4},{7,5},{8,10},{9,11},{10,... | collective-permute-start | bytes 24584 | tf_op jit(solution)/shard_map/ppermute | solution.py:270
  148.8 5.2 %collective-permute-start.17 = (f32[2048]{0:T(1024)S(1)}, f32[2048]{0:T(1024)S(1)}, u32[]{:S(2)}, u32[]{:S(2)}) collective-permute-start(f32[2048]{0:T(1024)S(1)} %add.310), channel_id=1, source_target_pairs={{0,4},{1,5},{2,6},{3,7},{4,0},{5,1},{6,2},{7,3},{8,12},{9,13},{10,... | collective-permute-start | bytes 24584 | tf_op jit(solution)/shard_map/ppermute | solution.py:270

commit v2 on v0

v2 whole, which is shorter than its diff:
```python
import math

import jax
import jax.numpy as jnp
from jax import lax
from jax.experimental import pallas as pl
from jax.experimental.pallas import tpu as pltpu
from jax.sharding import PartitionSpec as P

BLK = 256
LANES = 128
UNROLL = 8
TILES, LIVE = 0, 1


def inverse_norm(values):
    wide = values.astype(jnp.float32)
    return lax.rsqrt(jnp.mean(wide * wide, axis=-1) + 1e-06)


def pair_kernel(meta, q, iq, ic, fetched, out, sums, cbuf, acc, ring, zero, csem, osem):
    n_pairs = out.shape[0]
    n_src = cbuf.shape[0]
    depth = ring.shape[0]
    hi = meta[3, TILES]
    dead = meta[3, LIVE]

    def load(i):
        return pltpu.make_async_copy(fetched.at[pl.ds(i * BLK, BLK)], cbuf.at[i], csem.at[i])

    for i in range(n_src):
        load(i).start()
    zero[...] = jnp.zeros_like(zero)

    def zero_copy(j):
        return pltpu.make_async_copy(zero, out.at[meta[0, j]], osem.at[j])

    @pl.loop(dead, n_pairs)
    def _(j):
        zero_copy(j).start()

    acc[...] = jnp.zeros_like(acc)
    for i in range(n_src):
        load(i).wait()

    def score(t, slot, weight):
        qb = meta[1, t] % 8
        c = meta[1, t] // 8
        rows = pl.ds(pl.multiple_of(qb * BLK, BLK), BLK)
        dots = lax.dot_general(
            q[rows, :], cbuf[c], (((1,), (1,)), ((), ())), preferred_element_type=jnp.float32
        )
        inv_q = iq[rows, :]
        inv_c = ic[pl.ds(c, 1), :]
        total = None
        for h in range(BLK // LANES):
            cols = slice(h * LANES, (h + 1) * LANES)
            pos = jnp.maximum(dots[:, cols] * inv_q * inv_c[:, cols] - 1.0, 0.0)
            ring[slot, :, cols] = pos.astype(jnp.bfloat16)
            total = pos if total is None else total + pos
        acc[qb] += total * weight

    def tile_copies(t, slot, start):
        @pl.loop(meta[2, t], meta[2, t + 1])
        def _(j):
            copy = pltpu.make_async_copy(ring.at[slot], out.at[meta[0, j]], osem.at[j])
            copy.start() if start else copy.wait()

    rounds = depth // UNROLL
    steps = (hi + UNROLL - 1) // UNROLL

    @pl.loop(0, steps)
    def _(i):
        slot = lax.rem(i, rounds) * UNROLL
        a = UNROLL * i

        @pl.when(i >= rounds)
        def _():
            for u in range(UNROLL):
                tile_copies(a - depth + u, slot + u, False)

        for u in range(UNROLL):
            t = jnp.minimum(a + u, hi - 1)
            count = jnp.where(a + u < hi, meta[2, t + 1] - meta[2, t], 0)
            score(t, slot + u, count.astype(jnp.float32))
        for u in range(UNROLL):

            @pl.when(a + u < hi)
            def _():
                tile_copies(a + u, slot + u, True)

    for qb in range(acc.shape[0]):
        sums[qb : qb + 1, :] = jnp.sum(acc[qb].T, axis=0, keepdims=True)

    @pl.loop(jnp.maximum(0, UNROLL * (steps - rounds)), hi)
    def _(t):
        tile_copies(t, lax.rem(t, depth), False)

    @pl.loop(dead, n_pairs)
    def _(j):
        zero_copy(j).wait()


def score_pairs(n_pairs, meta, queries, inv_q, inv_c, fetched):
    n_src = fetched.shape[0] // BLK
    feature_dim = queries.shape[1]
    blocks = queries.shape[0] // BLK
    hbm = pl.BlockSpec(memory_space=pl.ANY)
    vmem = pl.BlockSpec(memory_space=pltpu.VMEM)
    return pl.pallas_call(
        pair_kernel,
        out_shape=(
            jax.ShapeDtypeStruct((n_pairs, BLK, BLK), jnp.bfloat16),
            jax.ShapeDtypeStruct((blocks, BLK), jnp.float32),
        ),
        in_specs=[pl.BlockSpec(memory_space=pltpu.SMEM), vmem, vmem, vmem, hbm],
        out_specs=(hbm, vmem),
        scratch_shapes=[
            pltpu.VMEM((n_src, BLK, feature_dim), jnp.bfloat16),
            pltpu.VMEM((blocks, BLK, LANES), jnp.float32),
            pltpu.VMEM((2 * UNROLL, BLK, BLK), jnp.bfloat16),
            pltpu.VMEM((BLK, BLK), jnp.bfloat16),
            pltpu.SemaphoreType.DMA((n_src,)),
            pltpu.SemaphoreType.DMA((n_pairs,)),
        ],
        cost_estimate=pl.CostEstimate(
            flops=2 * n_pairs * BLK * BLK * feature_dim,
            bytes_accessed=n_pairs * BLK * BLK * 2,
            transcendentals=0,
        ),
        compiler_params=pltpu.CompilerParams(vmem_limit_bytes=24 << 20),
        name="pairs",
    )(meta, queries, inv_q, inv_c, fetched)


def take_kernel(wanted, candidates, out, stage, sem):
    loads, stores = [], []
    for k in range(stage.shape[0]):
        block = candidates.at[pl.ds(pl.multiple_of(wanted[k] * BLK, BLK), BLK)]
        loads.append(pltpu.make_async_copy(block, stage.at[k], sem.at[0, k]))
        part = out.at[pl.ds(k * BLK, BLK)]
        stores.append(pltpu.make_async_copy(stage.at[k], part, sem.at[1, k]))
    for load in loads:
        load.start()
    for load, store in zip(loads, stores):
        load.wait()
        store.start()
    for store in stores:
        store.wait()


def take_blocks(wanted, candidates):
    count = wanted.shape[0]
    hbm = pl.BlockSpec(memory_space=pltpu.HBM)
    return pl.pallas_call(
        take_kernel,
        out_shape=pltpu.HBM((count * BLK, candidates.shape[1]), candidates.dtype),
        in_specs=[pl.BlockSpec(memory_space=pltpu.SMEM), hbm],
        out_specs=hbm,
        scratch_shapes=[
            pltpu.VMEM((count, BLK, candidates.shape[1]), candidates.dtype),
            pltpu.SemaphoreType.DMA((2, count)),
        ],
        compiler_params=pltpu.CompilerParams(vmem_limit_bytes=16 << 20),
        name="take",
    )(wanted, pltpu.with_memory_space_constraint(candidates, pltpu.HBM))


def per_device(queries, candidates, requests, pairs, counts):
    row_count = lax.axis_size("rows")
    col_count = lax.axis_size("cols")
    feature_dim = queries.shape[1]
    pair_count = pairs.shape[0]
    wanted = lax.all_to_all(requests, "rows", split_axis=0, concat_axis=0, tiled=True)[:, 0]
    sends = take_blocks(wanted, candidates)
    fetched = lax.all_to_all(sends, "rows", split_axis=0, concat_axis=0, tiled=True)
    queries, candidates, pairs, sends = lax.optimization_barrier(
        (queries, candidates, pairs, sends)
    )

    ids = jnp.arange(pair_count, dtype=jnp.int32)
    key = jnp.where(ids < counts[0], pairs[:, 1] * 8 + pairs[:, 0], row_count * 8)
    less = key[None, :] < key[:, None]
    twin = (key[None, :] == key[:, None]) & (ids[None, :] < ids[:, None])
    place = jnp.sum((less | twin).astype(jnp.int32), axis=1)
    lead = jnp.logical_not(jnp.any(twin, axis=1))
    tile = jnp.sum((less & lead[None, :]).astype(jnp.int32), axis=1)
    wide = jnp.arange(2 * pair_count, dtype=jnp.int32)
    at = place[None, :] == wide[:, None]
    sorted_ids = jnp.sum(jnp.where(at, ids[None, :], 0), axis=1)
    at = lead[None, :] & (tile[None, :] == wide[:, None])
    tile_key = jnp.sum(jnp.where(at, (key % (row_count * 8))[None, :], 0), axis=1)
    first_pair = jnp.sum(jnp.where(at, (place - pair_count)[None, :], 0), axis=1) + pair_count
    tiles = jnp.sum((lead & (ids < counts[0])).astype(jnp.int32))
    ends = jnp.where(wide == TILES, tiles, counts[0])
    meta = jnp.stack([sorted_ids, tile_key, first_pair, ends])

    inv_q = jnp.broadcast_to(inverse_norm(queries)[:, None], (queries.shape[0], LANES))
    norms = inverse_norm(candidates.reshape(-1, BLK, feature_dim)) * (1.0 / math.sqrt(feature_dim))
    norms = lax.all_gather(norms, "rows", axis=0, tiled=False)
    picked = requests == jnp.arange(norms.shape[1], dtype=jnp.int32)[None, :]
    inv_c = jnp.sum(jnp.where(picked[:, :, None], norms, 0.0), axis=1)

    out, local = score_pairs(pair_count, meta, queries, inv_q, inv_c, fetched)
    totals = local.reshape(-1)
    step = 1
    while step < col_count:
        totals = totals + lax.ppermute(totals, "cols", [(i, i ^ step) for i in range(col_count)])
        step *= 2
    return out, totals * (1.0 / BLK)


def solution(mesh):
    in_specs = (
        P("rows", None),
        P(("rows", "cols"), None),
        P(("rows", "cols"), None),
        P(("rows", "cols"), None),
        P(("rows", "cols")),
    )
    out_specs = (P(("rows", "cols"), None, None), P("rows"))
    return jax.shard_map(
        per_device, mesh=mesh, in_specs=in_specs, out_specs=out_specs, check_vma=False
    )
```

time: 410 us -> 174 us (0.42)
  the two profiles are of different devices: /device:TPU:80 before, /device:TPU:8 now
where the time goes in v2:
time: 174 us; the launch traced here: 171 us
  blocking collectives  120 us (69%)
  Pallas kernels  23.9 us (14%)
  starting transfers between devices  14.3 us (8%)
  other arithmetic  6.17 us (4%)
  waiting for transfers between devices  4.42 us (3%)
    all_gather x1, blocking collectives, per_device(): norms = lax.all_gather(norms, 'rows', axis=0, tiled=False)  105 us
    pallas_call x1, Pallas kernels, score_pairs(): pl.pallas_call(pair_kernel, out_shape=(jax.ShapeDtypeStruct((n_pairs, BLK...  17.6 us
    all_to_all x1, blocking collectives, per_device(): lax.all_to_all(requests, 'rows', split_axis=0, concat_axis=0, tiled=True)  14.4 us
    ppermute x3, starting transfers between devices, per_device(): lax.ppermute(totals, 'cols', [(i, i ^ step) for i in range(col_count)])  8.29 us
    pallas_call x1, Pallas kernels, take_blocks(): pl.pallas_call(take_kernel, out_shape=pltpu.HBM((count * BLK, candidates....  6.32 us
    all_to_all x1, starting transfers between devices, per_device(): lax.all_to_all(sends, 'rows', split_axis=0, concat_axis=0, tiled=True)  6.04 us
    ppermute x3, waiting for transfers between devices, per_device(): lax.ppermute(totals, 'cols', [(i, i ^ step) for i in range(col_count)])  4.41 us
  transfers between devices with their start and end apart: 4, of which 3 were waited for; matrix products, arithmetic and copies ran while one was open for 3% of the time, Pallas kernels for 0%

profile of v2, /device:TPU:8, one launch (start us, length us, event | category | flops | bytes accessed | tf_op | source)
XLA Modules:
  0.0 170.9 jit_solution(10819358983564223976)
XLA Ops:
  0.6 0.7 copy.9
  1.4 14.4 %all_to_all.20 = s32[16,1,1]{2,1,0:T(1,128)S(1)} all-to-all(s32[16,1,1]{2,1,0:T(1,128)S(1)} %copy.9), channel_id=1, replica_groups=mesh['rows'=16,'cols'=8] {'rows'}, dimensions={0} | all-to-all | bytes 128 | tf_op jit(solution)/shard_map/all_to_all | solution.py:174
  15.7 0.4 reduce.1.wanted
  16.1 6.3 %take.1 = bf16[4096,768]{1,0:T(8,128)(2,1)} custom-call(s32[16]{0:T(128)S(1)} %reduce.1.wanted, bf16[2048,768]{1,0:T(8,128)(2,1)} %candidates.1), custom_call_target="tpu_custom_call" | custom-call | tf_op jit(solution)/shard_map/take/pallas_call | solution.py:155
  22.4 0.0 copy-start.2
  22.5 0.0 copy-start.1
  22.5 0.0 copy-start
  22.5 6.0 %all-to-all-start.1 = ((bf16[16,256,768]{2,1,0:T(8,128)(2,1)}), bf16[16,256,768]{2,1,0:T(8,128)(2,1)}, u32[]{:S(2)}, u32[]{:S(2)}) async-start(bf16[16,256,768]{2,1,0:T(8,128)(2,1)} %bitcast.20), calls=%async_computation.1 | async-start | bytes 12582912 | tf_op jit(solution)/shard_map/all_to_all | solution.py:176
  29.2 0.0 copy-done.2
  29.2 0.1 iota_compare_fusion.3
  29.3 0.0 copy-done.1
  29.3 0.2 fusion.2
  29.5 0.0 copy-done
  29.5 3.2 %multiply_reduce_fusion = (f32[2048]{0:T(1024)S(1)}, f32[2048]{0:T(1024)S(1)}) fusion(bf16[2048,768]{1,0:T(8,128)(2,1)} %candidates.1, bf16[2048,768]{1,0:T(8,128)(2,1)S(1)} %copy-done), kind=kLoop, calls=%fused_computation | loop fusion | flops 9433088 | bytes 6307840 | tf_op jit(solution)/shard_map/reduce_sum | solution.py:18
  32.7 105.2 %all_gather.4 = f32[16,8,256]{2,1,0:T(8,128)S(1)} all-gather(f32[1,8,256]{2,1,0:T(8,128)S(1)} %mul.50), channel_id=1, replica_groups=mesh['rows'=16,'cols'=8] {'rows'}, dimensions={0}, use_global_device_ids=true | all-gather | bytes 139264 | tf_op jit(solution)/shard_map/all_gather | solution.py:200
  137.9 0.6 fusion.4
  138.5 0.6 compare_select_fusion
  139.1 0.2 convert_reduce_fusion
  139.3 0.2 select_reduce_fusion.2
  139.5 0.1 select_reduce_fusion.ic
  139.6 0.0 all-to-all-done.1
  139.6 0.3 broadcast_in_dim.81.iq
  140.0 17.6 %pairs.1 = (bf16[128,256,256]{2,1,0:T(8,128)(2,1)}, f32[8,256]{1,0:T(8,128)S(1)}) custom-call(s32[4,256]{1,0:T(4,128)S(1)} %pad_add_fusion.meta, bf16[2048,768]{1,0:T(8,128)(2,1)S(1)} %copy-done, f32[2048,128]{1,0:T(8,128)S(1)} %broadcast_in_dim.81.iq, f32[16,256]{1,0:T(8,128)S(1)} %select_reduce_fusion.ic, bf16[4096,768]{1,0:T(8,128)(2,1)} %bitcast.9.fetched), custom_call_target="tpu_custom_call" | custom-call | flops 12884901888 | bytes 16777216 | tf_op jit(solution)/shard_map/pairs/pallas_call | solution.py:110
  157.6 0.1 collective-permute-start
  157.7 1.2 collective-permute-done
  158.8 3.7 %collective-permute-start.1 = (f32[2048]{0:T(1024)S(1)}, f32[2048]{0:T(1024)S(1)}, u32[]{:S(2)}, u32[]{:S(2)}) collective-permute-start(f32[2048]{0:T(1024)S(1)} %add.85), channel_id=1, source_target_pairs={{0,2},{1,3},{2,0},{3,1},{4,6},{5,7},{6,4},{7,5},{8,10},{9,11},{10,... | collective-permute-start | bytes 24584 | tf_op jit(solution)/shard_map/ppermute | solution.py:208
  162.6 1.6 collective-permute-done.1
  164.2 4.5 %collective-permute-start.2 = (f32[2048]{0:T(1024)S(1)}, f32[2048]{0:T(1024)S(1)}, u32[]{:S(2)}, u32[]{:S(2)}) collective-permute-start(f32[2048]{0:T(1024)S(1)} %add.86), channel_id=1, source_target_pairs={{0,4},{1,5},{2,6},{3,7},{4,0},{5,1},{6,2},{7,3},{8,12},{9,13},{10,... | collective-permute-start | bytes 24584 | tf_op jit(solution)/shard_map/ppermute | solution.py:208
  168.7 1.6 collective-permute-done.2
  170.3 0.6 add_multiply_fusion
  (12 shorter events, 0.1 us)
Async XLA Ops:
  22.4 6.7 %copy-start.2 = (s32[16,1]{0,1:T(1,128)S(1)}, s32[16,1]{0,1:T(1,128)}, u32[]{:S(2)}) copy-start(s32[16,1]{0,1:T(1,128)} %param.7) | copy-start | bytes 196
  22.5 6.8 %copy-start.1 = (s32[128,2]{0,1:T(2,128)S(1)}, s32[128,2]{0,1:T(2,128)}, u32[]{:S(2)}) copy-start(s32[128,2]{0,1:T(2,128)} %param.8) | copy-start | bytes 3076
  22.5 7.0 %copy-start = (bf16[2048,768]{1,0:T(8,128)(2,1)S(1)}, bf16[2048,768]{1,0:T(8,128)(2,1)}, u32[]{:S(2)}) copy-start(bf16[2048,768]{1,0:T(8,128)(2,1)} %q) | copy-start | bytes 9437188
  22.5 117.2 %all-to-all-start.1 = ((bf16[16,256,768]{2,1,0:T(8,128)(2,1)}), bf16[16,256,768]{2,1,0:T(8,128)(2,1)}, u32[]{:S(2)}, u32[]{:S(2)}) async-start(bf16[16,256,768]{2,1,0:T(8,128)(2,1)} %bitcast.20), calls=%async_computation.1 | async-start | bytes 12582912 | tf_op jit(solution)/shard_map/all_to_all | solution.py:176
  157.6 1.3 collective-permute-start
  158.8 5.4 %collective-permute-start.1 = (f32[2048]{0:T(1024)S(1)}, f32[2048]{0:T(1024)S(1)}, u32[]{:S(2)}, u32[]{:S(2)}) collective-permute-start(f32[2048]{0:T(1024)S(1)} %add.85), channel_id=1, source_target_pairs={{0,2},{1,3},{2,0},{3,1},{4,6},{5,7},{6,4},{7,5},{8,10},{9,11},{10,... | collective-permute-start | bytes 24584 | tf_op jit(solution)/shard_map/ppermute | solution.py:208
  164.2 6.1 %collective-permute-start.2 = (f32[2048]{0:T(1024)S(1)}, f32[2048]{0:T(1024)S(1)}, u32[]{:S(2)}, u32[]{:S(2)}) collective-permute-start(f32[2048]{0:T(1024)S(1)} %add.86), channel_id=1, source_target_pairs={{0,4},{1,5},{2,6},{3,7},{4,0},{5,1},{6,2},{7,3},{8,12},{9,13},{10,... | collective-permute-start | bytes 24584 | tf_op jit(solution)/shard_map/ppermute | solution.py:208

commit v3 on v1

v3 whole, which is shorter than its diff:
```python
import functools
import math

import jax
import jax.numpy as jnp
from jax import lax
from jax.experimental import pallas as pl
from jax.experimental.pallas import tpu as pltpu
from jax.sharding import PartitionSpec as P

BLK = 256
LANES = 128
CALL_LIMIT = 32
HEAD = 5
ORDER = (
    (1, 1), (3, 3), (1, 3), (3, 1), (2, 0), (0, 2), (2, 1), (0, 3),
    (2, 3), (0, 1), (1, 2), (3, 0), (3, 2), (1, 0), (2, 2),
)
CALLS = ((0, 7, 8, 11), (7, 11, 8, 15), (11, 14, 8, 15), (14, 16, 4, 15))


def inverse_norm(values):
    wide = values.astype(jnp.float32)
    return lax.rsqrt(jnp.mean(wide * wide, axis=-1) + 1e-06)


def pair_kernel(call, n_src, unroll, zero_fill, feature_dim, meta, q, iq, *refs):
    srcs = refs[:n_src]
    out, sums, cbuf, ic, acc, ring, zero, csem, osem = refs[-9:]
    n_pairs = out.shape[0]
    depth = ring.shape[0]
    lo = meta[3, call]
    hi = meta[3, call + 1]
    copies = [pltpu.make_async_copy(srcs[i], cbuf.at[i], csem.at[i]) for i in range(n_src)]
    for copy in copies:
        copy.start()
    acc[...] = jnp.zeros_like(acc)
    if zero_fill:
        zero[...] = jnp.zeros_like(zero)
        dead = meta[3, CALL_LIMIT]

        def zero_copy(j):
            return pltpu.make_async_copy(zero, out.at[meta[0, j]], osem.at[j])

        @pl.loop(dead, n_pairs)
        def _(j):
            zero_copy(j).start()

    dims = (((1,), (1,)), ((), ()))
    scale = 1.0 / math.sqrt(feature_dim)
    for i in range(n_src):
        copies[i].wait()
        squares = None
        for h in range(feature_dim // LANES):
            wide = cbuf[i, :, h * LANES : (h + 1) * LANES].astype(jnp.float32)
            squares = wide * wide if squares is None else squares + wide * wide
        total = jnp.sum(squares.T, axis=0, keepdims=True)
        ic[i] = lax.rsqrt(total * (1.0 / feature_dim) + 1e-06) * scale

    def score(t, slot, weight):
        qb = meta[1, t] % 8
        c = meta[1, t] // 8
        rows = pl.ds(pl.multiple_of(qb * BLK, BLK), BLK)
        dots = lax.dot_general(q[rows, :], cbuf[c], dims, preferred_element_type=jnp.float32)
        inv_q = iq[rows, :]
        inv_c = ic[c]
        total = None
        for h in range(BLK // LANES):
            cols = slice(h * LANES, (h + 1) * LANES)
            pos = jnp.maximum(dots[:, cols] * inv_q * inv_c[:, cols] - 1.0, 0.0)
            ring[slot, :, cols] = pos.astype(jnp.bfloat16)
            total = pos if total is None else total + pos
        acc[qb] += total * weight

    def tile_copies(t, slot, start):
        @pl.loop(meta[2, t], meta[2, t + 1])
        def _(j):
            copy = pltpu.make_async_copy(ring.at[slot], out.at[meta[0, j]], osem.at[j])
            copy.start() if start else copy.wait()

    rounds = depth // unroll
    steps = (hi - lo + unroll - 1) // unroll

    @pl.loop(0, steps)
    def _(i):
        slot = lax.rem(i, rounds) * unroll
        a = lo + unroll * i

        @pl.when(i >= rounds)
        def _():
            for u in range(unroll):
                tile_copies(a - depth + u, slot + u, False)

        for u in range(unroll):
            t = jnp.minimum(a + u, hi - 1)
            count = jnp.where(a + u < hi, meta[2, t + 1] - meta[2, t], 0)
            score(t, slot + u, count.astype(jnp.float32))
        for u in range(unroll):

            @pl.when(a + u < hi)
            def _():
                tile_copies(a + u, slot + u, True)

    @pl.loop(jnp.maximum(lo, lo + unroll * (steps - rounds)), hi)
    def _(t):
        tile_copies(t, lax.rem(t - lo, depth), False)

    if zero_fill:

        @pl.loop(dead, n_pairs)
        def _(j):
            zero_copy(j).wait()

    for qb in range(acc.shape[0]):
        sums[qb : qb + 1, :] = jnp.sum(acc[qb].T, axis=0, keepdims=True)


def take_kernel(codes, wanted, to, candidates, *refs):
    outs, sem = refs[:-1], refs[-1]
    copies = []
    for i, code in enumerate(codes):
        start = pl.multiple_of(wanted[to[code]] * BLK, BLK)
        copies.append(
            pltpu.make_async_copy(candidates.at[pl.ds(start, BLK)], outs[i], sem.at[i])
        )
    for copy in copies:
        copy.start()
    for copy in copies:
        copy.wait()


def take_blocks(offsets, wanted, to, candidates):
    side = math.isqrt(to.shape[0])
    smem = pl.BlockSpec(memory_space=pltpu.SMEM)
    hbm = pl.BlockSpec(memory_space=pl.ANY)
    codes = tuple(dy * side + dz for dy, dz in offsets)
    return list(
        pl.pallas_call(
            functools.partial(take_kernel, codes),
            out_shape=(
                jax.ShapeDtypeStruct((BLK, candidates.shape[1]), candidates.dtype),
            )
            * len(codes),
            in_specs=[smem, smem, pl.BlockSpec(memory_space=pltpu.HBM)],
            out_specs=(hbm,) * len(codes),
            scratch_shapes=[pltpu.SemaphoreType.DMA((len(codes),))],
            compiler_params=pltpu.CompilerParams(vmem_limit_bytes=1 << 20),
            name="take_%d" % len(codes),
        )(wanted, to, pltpu.with_memory_space_constraint(candidates, pltpu.HBM))
    )


def score_pairs(call, unroll, sources, zero_fill, n_pairs, meta, queries, inv_q, *out):
    n_src = len(sources)
    feature_dim = queries.shape[1]
    blocks = queries.shape[0] // BLK
    pairs_here = max(n_pairs * n_src // 16, 1)
    hbm = pl.BlockSpec(memory_space=pl.ANY)
    vmem = pl.BlockSpec(memory_space=pltpu.VMEM)
    return pl.pallas_call(
        functools.partial(pair_kernel, call, n_src, unroll, zero_fill, feature_dim),
        out_shape=(
            jax.ShapeDtypeStruct((n_pairs, BLK, BLK), jnp.bfloat16),
            jax.ShapeDtypeStruct((blocks, BLK), jnp.float32),
        ),
        in_specs=[pl.BlockSpec(memory_space=pltpu.SMEM), vmem, vmem]
        + [hbm] * (n_src + len(out)),
        out_specs=(hbm, vmem),
        scratch_shapes=[
            pltpu.VMEM((n_src, BLK, feature_dim), jnp.bfloat16),
            pltpu.VMEM((n_src, 1, BLK), jnp.float32),
            pltpu.VMEM((blocks, BLK, LANES), jnp.float32),
            pltpu.VMEM((2 * unroll, BLK, BLK), jnp.bfloat16),
            pltpu.VMEM((BLK, BLK), jnp.bfloat16),
            pltpu.SemaphoreType.DMA((n_src,)),
            pltpu.SemaphoreType.DMA((n_pairs,)),
        ],
        input_output_aliases={3 + n_src: 0} if out else {},
        cost_estimate=pl.CostEstimate(
            flops=2 * pairs_here * BLK * BLK * feature_dim,
            bytes_accessed=pairs_here * BLK * BLK * 2,
            transcendentals=0,
        ),
        compiler_params=pltpu.CompilerParams(vmem_limit_bytes=12 << 20),
        name="pairs_%d" % call,
    )(meta, queries, inv_q, *sources, *out)


def per_device(queries, candidates, requests, pairs, counts):
    row_count = lax.axis_size("rows")
    side = math.isqrt(row_count)
    col_count = lax.axis_size("cols")
    feature_dim = queries.shape[1]
    pair_count = pairs.shape[0]
    me = lax.axis_index("rows")
    my_y, my_z = me // side, me % side
    wanted = lax.all_to_all(requests, "rows", split_axis=0, concat_axis=0, tiled=True)[:, 0]

    offsets = ((0, 0),) + ORDER
    key_of = [0] * row_count
    for call, (lo, hi, _, _) in enumerate(CALLS):
        for rank in range(lo, hi):
            dy, dz = offsets[rank]
            key_of[dy * side + dz] = (call * row_count + rank - lo) * 8
    slots = pairs[:, 1]
    away = ((my_y - slots // side) % side) * side + (my_z - slots % side) % side
    ids = jnp.arange(pair_count, dtype=jnp.int32)
    key = pairs[:, 0]
    for code, value in enumerate(key_of):
        key = key + jnp.where(away == code, value, 0)
    key = jnp.where(ids < counts[0], key, CALL_LIMIT * row_count * 8)
    less = key[None, :] < key[:, None]
    twin = (key[None, :] == key[:, None]) & (ids[None, :] < ids[:, None])
    place = jnp.sum((less | twin).astype(jnp.int32), axis=1)
    lead = jnp.logical_not(jnp.any(twin, axis=1))
    tile = jnp.sum((less & lead[None, :]).astype(jnp.int32), axis=1)
    wide = jnp.arange(2 * pair_count, dtype=jnp.int32)
    at = place[None, :] == wide[:, None]
    sorted_ids = jnp.sum(jnp.where(at, ids[None, :], 0), axis=1)
    at = lead[None, :] & (tile[None, :] == wide[:, None])
    tile_key = jnp.sum(jnp.where(at, (key % (row_count * 8))[None, :], 0), axis=1)
    first_pair = jnp.sum(jnp.where(at, (place - pair_count)[None, :], 0), axis=1) + pair_count
    below = lead[None, :] & (key[None, :] < (wide * (row_count * 8))[:, None])
    starts = jnp.sum(below.astype(jnp.int32), axis=1)
    starts = jnp.where(wide == CALL_LIMIT, counts[0], starts)
    meta = jnp.stack([sorted_ids, tile_key, first_pair, starts])

    codes = jnp.arange(row_count, dtype=jnp.int32)
    to = ((my_y + codes // side) % side) * side + (my_z + codes % side) % side
    sends = take_blocks(ORDER[:HEAD], wanted, to, candidates)
    arrived = [None]
    out, sums, scored = None, [], 0

    def score(out, scored):
        lo, hi, unroll, _ = CALLS[scored]
        out, part = score_pairs(
            scored, unroll, arrived[lo:hi], scored == 0, pair_count, meta, queries, inv_q,
            *(() if out is None else (out,)),
        )
        sums.append(part)
        return out

    for k, (dy, dz) in enumerate(ORDER):
        if k == HEAD:
            to = lax.optimization_barrier((to, arrived[1]))[0]
            sends += take_blocks(ORDER[HEAD:] + ((0, 0),), wanted, to, candidates)
            arrived[0] = sends.pop()
            inv_q = inverse_norm(lax.optimization_barrier((queries, arrived[1]))[0])
            inv_q = jnp.broadcast_to(inv_q[:, None], (queries.shape[0], LANES))
        send = sends[k]
        if scored < len(CALLS) and CALLS[scored][3] == k:
            out = score(out, scored)
            scored += 1
        if sums:
            send = lax.optimization_barrier((send, sums[-1]))[0]
        perm = [
            (y * side + z, ((y + dy) % side) * side + (z + dz) % side)
            for y in range(side)
            for z in range(side)
        ]
        arrived.append(lax.ppermute(send, "rows", perm))
    while scored < len(CALLS):
        out = score(out, scored)
        scored += 1
    local = functools.reduce(jnp.add, sums)
    totals = local.reshape(-1)

    def other(values, flip):
        return lax.ppermute(values, "cols", [(i, i ^ flip) for i in range(col_count)])

    totals = totals + other(totals, 1)
    totals = (totals + other(totals, 2)) + (other(totals, 4) + other(totals, 6))
    return out, totals * (1.0 / BLK)


def solution(mesh):
    in_specs = (
        P("rows", None),
        P(("rows", "cols"), None),
        P(("rows", "cols"), None),
        P(("rows", "cols"), None),
        P(("rows", "cols")),
    )
    out_specs = (P(("rows", "cols"), None, None), P("rows"))
    return jax.shard_map(
        per_device, mesh=mesh, in_specs=in_specs, out_specs=out_specs, check_vma=False
    )
```

time: 155 us -> 129 us (0.83)
  the two profiles are of different devices: /device:TPU:68 before, /device:TPU:8 now
where the time goes in v3:
time: 129 us
  starting transfers between devices  58.1 us (45%)
  waiting for transfers between devices  32.1 us (25%)
  Pallas kernels  31.3 us (24%)
  other arithmetic  3.95 us (3%)
  local copies, waits for them, and re-layouts  1.81 us (1%)
  between operations  1.52 us (1%)
    ppermute x15, starting transfers between devices, per_device(): arrived.append(lax.ppermute(send, 'rows', perm))  37.7 us
    pallas_call x4, Pallas kernels, score_pairs(): pl.pallas_call(functools.partial(pair_kernel, call, n_src, unroll, zero_f...  26.3 us
    ppermute x15, waiting for transfers between devices, per_device(): arrived.append(lax.ppermute(send, 'rows', perm))  23.8 us
    ppermute x4, starting transfers between devices, other(): lax.ppermute(values, 'cols', [(i, i ^ flip) for i in range(col_count)])  12 us
    all_to_all x1, starting transfers between devices, per_device(): lax.all_to_all(requests, 'rows', split_axis=0, concat_axis=0, tiled=True)  8.41 us
    ppermute x4, waiting for transfers between devices, other(): lax.ppermute(values, 'cols', [(i, i ^ flip) for i in range(col_count)])  5.1 us
    pallas_call x2, Pallas kernels, take_blocks(): pl.pallas_call(functools.partial(take_kernel, codes), out_shape=(jax.Shap...  5.02 us
    all_to_all x1, waiting for transfers between devices, per_device(): lax.all_to_all(requests, 'rows', split_axis=0, concat_axis=0, tiled=True)  3.17 us
  transfers between devices with their start and end apart: 20, of which 9 were waited for; matrix products, arithmetic and copies ran while one was open for 3% of the time, Pallas kernels for 19%

profile of v3, /device:TPU:8, one launch (start us, length us, event | category | flops | bytes accessed | tf_op | source)
XLA Modules:
  0.0 128.7 jit_solution(2905000866028143133)
XLA Ops:
  0.6 1.5 %copy.12 = s32[16,1,1]{2,1,0:T(1,128)} copy(s32[16,1,1]{0,2,1:T(1,128)} %bitcast.37) | data formatting | bytes 128 | tf_op jit(solution)/shard_map/all_to_all | solution.py:197
  2.1 8.4 %all-to-all-start = ((s32[16,1,1]{2,1,0:T(1,128)}), s32[16,1,1]{2,1,0:T(1,128)S(1)}, u32[]{:S(2)}, u32[]{:S(2)}) async-start(s32[16,1,1]{2,1,0:T(1,128)} %copy.12), calls=%async_computation | async-start | bytes 16384 | tf_op jit(solution)/shard_map/all_to_all | solution.py:197
  11.2 0.8 fusion.25
  12.0 0.8 and_select_fusion.4
  13.5 3.2 %all-to-all-done = s32[16,1,1]{2,1,0:T(1,128)S(1)} async-done(((s32[16,1,1]{2,1,0:T(1,128)}), s32[16,1,1]{2,1,0:T(1,128)S(1)}, u32[]{:S(2)}, u32[]{:S(2)}) %all-to-all-start) | async-done | bytes 96 | tf_op jit(solution)/shard_map/all_to_all | solution.py:197
  17.0 2.1 %take_5.1 = (bf16[256,768]{1,0:T(8,128)(2,1)S(1)}, bf16[256,768]{1,0:T(8,128)(2,1)S(1)}, bf16[256,768]{1,0:T(8,128)(2,1)S(1)}, bf16[256,768]{1,0:T(8,128)(2,1)S(1)}, bf16[256,768]{1,0:T(8,128)(2,1)S(1)}) custom-call(s32[16]{0:T(128)S(1)} %reduce.wanted, s32[16]{0:T(128)S(1)} %fusion.6.to, bf16[2048,768]{1,0:T(8,128)(2,1)} %candidates.3), custom_call_target="tpu_custom_call" | custom-call | tf_op jit(solution)/shard_map/take_5/pallas_call | solution.py:138
  19.2 0.6 collective-permute-start
  19.8 3.7 %collective-permute-start.1 = (bf16[256,768]{1,0:T(8,128)(2,1)S(1)}, bf16[256,768]{1,0:T(8,128)(2,1)S(1)}, u32[]{:S(2)}, u32[]{:S(2)}) collective-permute-start(bf16[256,768]{1,0:T(8,128)(2,1)S(1)} %get-tuple-element.37), channel_id=1, source_target_pairs={{0,120},{8,96},{16,104},{24,112},{32,24},{40,0},{48,8},{56,16},{64... | collective-permute-start | bytes 1179656 | tf_op jit(solution)/shard_map/ppermute | solution.py:261
  23.5 2.9 %collective-permute-start.3 = (bf16[256,768]{1,0:T(8,128)(2,1)S(1)}, bf16[256,768]{1,0:T(8,128)(2,1)S(1)}, u32[]{:S(2)}, u32[]{:S(2)}) collective-permute-start(bf16[256,768]{1,0:T(8,128)(2,1)S(1)} %get-tuple-element.39), channel_id=1, source_target_pairs={{0,104},{8,112},{16,120},{24,96},{32,8},{40,16},{48,24},{56,0},{64... | collective-permute-start | bytes 1179656 | tf_op jit(solution)/shard_map/ppermute | solution.py:261
  26.4 1.4 %collective-permute-start.4 = (bf16[256,768]{1,0:T(8,128)(2,1)S(1)}, bf16[256,768]{1,0:T(8,128)(2,1)S(1)}, u32[]{:S(2)}, u32[]{:S(2)}) collective-permute-start(bf16[256,768]{1,0:T(8,128)(2,1)S(1)} %get-tuple-element.40), channel_id=1, source_target_pairs={{0,64},{8,72},{16,80},{24,88},{32,96},{40,104},{48,112},{56,120},{... | collective-permute-start | bytes 1179656 | tf_op jit(solution)/shard_map/ppermute | solution.py:261
  27.8 5.6 %collective-permute-done.refs_1_ = bf16[256,768]{1,0:T(8,128)(2,1)S(1)} collective-permute-done((bf16[256,768]{1,0:T(8,128)(2,1)S(1)}, bf16[256,768]{1,0:T(8,128)(2,1)S(1)}, u32[]{:S(2)}, u32[]{:S(2)}) %collective-permute-start) | collective-permute-done | bytes 393248 | tf_op jit(solution)/shard_map/ppermute | solution.py:261
  33.4 2.9 %take_11.1 = (bf16[256,768]{1,0:T(8,128)(2,1)S(1)}, bf16[256,768]{1,0:T(8,128)(2,1)S(1)}, bf16[256,768]{1,0:T(8,128)(2,1)S(1)}, bf16[256,768]{1,0:T(8,128)(2,1)S...) custom-call(s32[16]{0:T(128)S(1)} %reduce.wanted, ...), custom_call_target="tpu_custom_call" | custom-call | tf_op jit(solution)/shard_map/take_11/pallas_call | solution.py:138
  36.4 0.7 multiply_reduce_fusion
  37.1 3.5 %collective-permute-start.8 = (bf16[256,768]{1,0:T(8,128)(2,1)S(1)}, bf16[256,768]{1,0:T(8,128)(2,1)S(1)}, u32[]{:S(2)}, u32[]{:S(2)}) collective-permute-start(bf16[256,768]{1,0:T(8,128)(2,1)S(1)} %get-tuple-element.46), channel_id=1, source_target_pairs={{0,48},{8,56},{16,32},{24,40},{32,80},{40,88},{48,64},{56,72},{64,... | collective-permute-start | bytes 1179656 | tf_op jit(solution)/shard_map/ppermute | solution.py:261
  40.6 7.7 %collective-permute-done.2.refs_3_ = bf16[256,768]{1,0:T(8,128)(2,1)S(1)} collective-permute-done((bf16[256,768]{1,0:T(8,128)(2,1)S(1)}, bf16[256,768]{1,0:T(8,128)(2,1)S(1)}, u32[]{:S(2)}, u32[]{:S(2)}) %collective-permute-start.2) | collective-permute-done | bytes 393248 | tf_op jit(solution)/shard_map/ppermute | solution.py:261
  48.3 2.0 %collective-permute-start.12 = (bf16[256,768]{1,0:T(8,128)(2,1)S(1)}, bf16[256,768]{1,0:T(8,128)(2,1)S(1)}, u32[]{:S(2)}, u32[]{:S(2)}) collective-permute-start(bf16[256,768]{1,0:T(8,128)(2,1)S(1)} %get-tuple-element.52), channel_id=1, source_target_pairs={{0,24},{8,0},{16,8},{24,16},{32,56},{40,32},{48,40},{56,48},{64,88... | collective-permute-start | bytes 1179656 | tf_op jit(solution)/shard_map/ppermute | solution.py:261
  50.4 2.9 %collective-permute-done.4.refs_5_ = bf16[256,768]{1,0:T(8,128)(2,1)S(1)} collective-permute-done((bf16[256,768]{1,0:T(8,128)(2,1)S(1)}, bf16[256,768]{1,0:T(8,128)(2,1)S(1)}, u32[]{:S(2)}, u32[]{:S(2)}) %collective-permute-start.4) | collective-permute-done | bytes 393248 | tf_op jit(solution)/shard_map/ppermute | solution.py:261
  53.3 15.5 %collective-permute-start.13 = (bf16[256,768]{1,0:T(8,128)(2,1)S(1)}, bf16[256,768]{1,0:T(8,128)(2,1)S(1)}, u32[]{:S(2)}, u32[]{:S(2)}) collective-permute-start(bf16[256,768]{1,0:T(8,128)(2,1)S(1)} %get-tuple-element.53), channel_id=1, source_target_pairs={{0,88},{8,64},{16,72},{24,80},{32,120},{40,96},{48,104},{56,112},{... | collective-permute-start | bytes 1179656 | tf_op jit(solution)/shard_map/ppermute | solution.py:261
  69.1 9.8 %pairs_0.1 = (bf16[128,256,256]{2,1,0:T(8,128)(2,1)}, f32[8,256]{1,0:T(8,128)S(1)}) custom-call(s32[4,256]{1,0:T(4,128)S(1)} %pad_add_fusion.meta, bf16[2048,768]{1,0:T(8,128)(2,1)S(1)} %copy-done, f32[2048,128]{1,0:T(8,128)S(1)} %broadcast_in_dim.189.iq, bf16[256,768]{1,0:T(8,128)(2,1)S(1)} %get-tuple-element.36.refs_0_, ...), custom_call_target="tpu_custom_call" | custom-call | flops 5637144576 | bytes 7340032 | tf_op jit(solution)/shard_map/pairs_0/pallas_call | solution.py:160
  79.0 4.3 %collective-permute-start.10 = (bf16[256,768]{1,0:T(8,128)(2,1)S(1)}, bf16[256,768]{1,0:T(8,128)(2,1)S(1)}, u32[]{:S(2)}, u32[]{:S(2)}) collective-permute-start(bf16[256,768]{1,0:T(8,128)(2,1)S(1)} %get-tuple-element.50), channel_id=1, source_target_pairs={{0,112},{8,120},{16,96},{24,104},{32,16},{40,24},{48,0},{56,8},{64... | collective-permute-start | bytes 1179656 | tf_op jit(solution)/shard_map/ppermute | solution.py:261
  83.3 3.2 %collective-permute-start.6 = (bf16[256,768]{1,0:T(8,128)(2,1)S(1)}, bf16[256,768]{1,0:T(8,128)(2,1)S(1)}, u32[]{:S(2)}, u32[]{:S(2)}) collective-permute-start(bf16[256,768]{1,0:T(8,128)(2,1)S(1)} %get-tuple-element.43), channel_id=1, source_target_pairs={{0,32},{8,40},{16,48},{24,56},{32,64},{40,72},{48,80},{56,88},{64,... | collective-permute-start | bytes 1179656 | tf_op jit(solution)/shard_map/ppermute | solution.py:261
  86.5 0.5 collective-permute-start.7
  86.9 7.0 %pairs_1.1 = (bf16[128,256,256]{2,1,0:T(8,128)(2,1)}, f32[8,256]{1,0:T(8,128)S(1)}) custom-call(s32[4,256]{1,0:T(4,128)S(1)} %pad_add_fusion.meta, bf16[2048,768]{1,0:T(8,128)(2,1)S(1)} %copy-done, f32[2048,128]{1,0:T(8,128)S(1)} %broadcast_in_dim.189.iq, bf16[256,768]{1,0:T(8,128)(2,1)S(1)} %collective-permute-done.11.refs_0_, ...), custom_call_target="tpu_custom_call", output_to_operand_aliasing={{0}: (7, {})} | custom-call | flops 3221225472 | bytes 4194304 | tf_op jit(solution)/shard_map/pairs_1/pallas_call | solution.py:160
  93.9 5.3 %collective-permute-done.10.refs_2_ = bf16[256,768]{1,0:T(8,128)(2,1)S(1)} collective-permute-done((bf16[256,768]{1,0:T(8,128)(2,1)S(1)}, bf16[256,768]{1,0:T(8,128)(2,1)S(1)}, u32[]{:S(2)}, u32[]{:S(2)}) %collective-permute-start.10) | collective-permute-done | bytes 393248 | tf_op jit(solution)/shard_map/ppermute | solution.py:261
  99.2 5.1 %pairs_2.1 = (bf16[128,256,256]{2,1,0:T(8,128)(2,1)}, f32[8,256]{1,0:T(8,128)S(1)}) custom-call(s32[4,256]{1,0:T(4,128)S(1)} %pad_add_fusion.meta, bf16[2048,768]{1,0:T(8,128)(2,1)S(1)} %copy-done, f32[2048,128]{1,0:T(8,128)S(1)} %broadcast_in_dim.189.iq, bf16[256,768]{1,0:T(8,128)(2,1)S(1)} %collective-permute-done.8.refs_0_, ...), custom_call_target="tpu_custom_call", output_to_operand_aliasing={{0}: (6, {})} | custom-call | flops 2415919104 | bytes 3145728 | tf_op jit(solution)/shard_map/pairs_2/pallas_call | solution.py:160
  104.3 2.2 %collective-permute-done.7.refs_1_ = bf16[256,768]{1,0:T(8,128)(2,1)S(1)} collective-permute-done((bf16[256,768]{1,0:T(8,128)(2,1)S(1)}, bf16[256,768]{1,0:T(8,128)(2,1)S(1)}, u32[]{:S(2)}, u32[]{:S(2)}) %collective-permute-start.7) | collective-permute-done | bytes 393248 | tf_op jit(solution)/shard_map/ppermute | solution.py:261
  106.6 4.4 %pairs_3.1 = (bf16[128,256,256]{2,1,0:T(8,128)(2,1)}, f32[8,256]{1,0:T(8,128)S(1)}) custom-call(s32[4,256]{1,0:T(4,128)S(1)} %pad_add_fusion.meta, bf16[2048,768]{1,0:T(8,128)(2,1)S(1)} %copy-done, f32[2048,128]{1,0:T(8,128)S(1)} %broadcast_in_dim.189.iq, bf16[256,768]{1,0:T(8,128)(2,1)S(1)} %collective-permute-done.6.refs_0_, ...), custom_call_target="tpu_custom_call", output_to_operand_aliasing={{0}: (5, {})} | custom-call | flops 1610612736 | bytes 2097152 | tf_op jit(solution)/shard_map/pairs_3/pallas_call | solution.py:160
  111.1 1.2 collective-permute-done.15
  112.2 10.7 %collective-permute-start.18 = (f32[2048]{0:T(1024)S(1)}, f32[2048]{0:T(1024)S(1)}, u32[]{:S(2)}, u32[]{:S(2)}) collective-permute-start(f32[2048]{0:T(1024)S(1)} %add.409), channel_id=1, source_target_pairs={{0,6},{1,7},{2,4},{3,5},{4,2},{5,3},{6,0},{7,1},{8,14},{9,15},{10,... | collective-permute-start | bytes 24584 | tf_op jit(solution)/shard_map/ppermute | solution.py:269
  122.9 1.2 collective-permute-start.17
  124.6 3.5 %collective-permute-done.17 = f32[2048]{0:T(1024)S(1)} collective-permute-done((f32[2048]{0:T(1024)S(1)}, f32[2048]{0:T(1024)S(1)}, u32[]{:S(2)}, u32[]{:S(2)}) %collective-permute-start.17) | collective-permute-done | bytes 8224 | tf_op jit(solution)/shard_map/ppermute | solution.py:269
  128.1 0.6 add_multiply_fusion
  (37 shorter events, 2.1 us)
Async XLA Ops:
  0.6 35.8 %copy-start = (bf16[2048,768]{1,0:T(8,128)(2,1)S(1)}, bf16[2048,768]{1,0:T(8,128)(2,1)}, u32[]{:S(2)}) copy-start(bf16[2048,768]{1,0:T(8,128)(2,1)} %q.7) | copy-start | bytes 9437188
  2.1 14.5 %all-to-all-start = ((s32[16,1,1]{2,1,0:T(1,128)}), s32[16,1,1]{2,1,0:T(1,128)S(1)}, u32[]{:S(2)}, u32[]{:S(2)}) async-start(s32[16,1,1]{2,1,0:T(1,128)} %copy.12), calls=%async_computation | async-start | bytes 16384 | tf_op jit(solution)/shard_map/all_to_all | solution.py:197
  19.2 14.2 %collective-permute-start = (bf16[256,768]{1,0:T(8,128)(2,1)S(1)}, bf16[256,768]{1,0:T(8,128)(2,1)S(1)}, u32[]{:S(2)}, u32[]{:S(2)}) collective-permute-start(bf16[256,768]{1,0:T(8,128)(2,1)S(1)} %get-tuple-element.32), channel_id=1, source_target_pairs={{0,40},{8,48},{16,56},{24,32},{32,72},{40,80},{48,88},{56,64},{64,... | collective-permute-start | bytes 1179656 | tf_op jit(solution)/shard_map/ppermute | solution.py:261
  19.8 17.3 %collective-permute-start.1 = (bf16[256,768]{1,0:T(8,128)(2,1)S(1)}, bf16[256,768]{1,0:T(8,128)(2,1)S(1)}, u32[]{:S(2)}, u32[]{:S(2)}) collective-permute-start(bf16[256,768]{1,0:T(8,128)(2,1)S(1)} %get-tuple-element.37), channel_id=1, source_target_pairs={{0,120},{8,96},{16,104},{24,112},{32,24},{40,0},{48,8},{56,16},{64... | collective-permute-start | bytes 1179656 | tf_op jit(solution)/shard_map/ppermute | solution.py:261
  23.5 24.9 %collective-permute-start.2 = (bf16[256,768]{1,0:T(8,128)(2,1)S(1)}, bf16[256,768]{1,0:T(8,128)(2,1)S(1)}, u32[]{:S(2)}, u32[]{:S(2)}) collective-permute-start(bf16[256,768]{1,0:T(8,128)(2,1)S(1)} %get-tuple-element.38), channel_id=1, source_target_pairs={{0,56},{8,32},{16,40},{24,48},{32,88},{40,64},{48,72},{56,80},{64,... | collective-permute-start | bytes 1179656 | tf_op jit(solution)/shard_map/ppermute | solution.py:261
  23.5 24.9 %collective-permute-start.3 = (bf16[256,768]{1,0:T(8,128)(2,1)S(1)}, bf16[256,768]{1,0:T(8,128)(2,1)S(1)}, u32[]{:S(2)}, u32[]{:S(2)}) collective-permute-start(bf16[256,768]{1,0:T(8,128)(2,1)S(1)} %get-tuple-element.39), channel_id=1, source_target_pairs={{0,104},{8,112},{16,120},{24,96},{32,8},{40,16},{48,24},{56,0},{64... | collective-permute-start | bytes 1179656 | tf_op jit(solution)/shard_map/ppermute | solution.py:261
  26.4 26.9 %collective-permute-start.4 = (bf16[256,768]{1,0:T(8,128)(2,1)S(1)}, bf16[256,768]{1,0:T(8,128)(2,1)S(1)}, u32[]{:S(2)}, u32[]{:S(2)}) collective-permute-start(bf16[256,768]{1,0:T(8,128)(2,1)S(1)} %get-tuple-element.40), channel_id=1, source_target_pairs={{0,64},{8,72},{16,80},{24,88},{32,96},{40,104},{48,112},{56,120},{... | collective-permute-start | bytes 1179656 | tf_op jit(solution)/shard_map/ppermute | solution.py:261
  36.3 32.5 %collective-permute-start.5 = (bf16[256,768]{1,0:T(8,128)(2,1)S(1)}, bf16[256,768]{1,0:T(8,128)(2,1)S(1)}, u32[]{:S(2)}, u32[]{:S(2)}) collective-permute-start(bf16[256,768]{1,0:T(8,128)(2,1)S(1)} %get-tuple-element.41), channel_id=1, source_target_pairs={{0,16},{8,24},{16,0},{24,8},{32,48},{40,56},{48,32},{56,40},{64,80... | collective-permute-start | bytes 1179656 | tf_op jit(solution)/shard_map/ppermute | solution.py:261
  37.1 56.8 %collective-permute-start.8 = (bf16[256,768]{1,0:T(8,128)(2,1)S(1)}, bf16[256,768]{1,0:T(8,128)(2,1)S(1)}, u32[]{:S(2)}, u32[]{:S(2)}) collective-permute-start(bf16[256,768]{1,0:T(8,128)(2,1)S(1)} %get-tuple-element.46), channel_id=1, source_target_pairs={{0,48},{8,56},{16,32},{24,40},{32,80},{40,88},{48,64},{56,72},{64,... | collective-permute-start | bytes 1179656 | tf_op jit(solution)/shard_map/ppermute | solution.py:261
  48.3 30.6 %collective-permute-start.11 = (bf16[256,768]{1,0:T(8,128)(2,1)S(1)}, bf16[256,768]{1,0:T(8,128)(2,1)S(1)}, u32[]{:S(2)}, u32[]{:S(2)}) collective-permute-start(bf16[256,768]{1,0:T(8,128)(2,1)S(1)} %get-tuple-element.51), channel_id=1, source_target_pairs={{0,72},{8,80},{16,88},{24,64},{32,104},{40,112},{48,120},{56,96},{... | collective-permute-start | bytes 1179656 | tf_op jit(solution)/shard_map/ppermute | solution.py:261
  48.3 30.7 %collective-permute-start.12 = (bf16[256,768]{1,0:T(8,128)(2,1)S(1)}, bf16[256,768]{1,0:T(8,128)(2,1)S(1)}, u32[]{:S(2)}, u32[]{:S(2)}) collective-permute-start(bf16[256,768]{1,0:T(8,128)(2,1)S(1)} %get-tuple-element.52), channel_id=1, source_target_pairs={{0,24},{8,0},{16,8},{24,16},{32,56},{40,32},{48,40},{56,48},{64,88... | collective-permute-start | bytes 1179656 | tf_op jit(solution)/shard_map/ppermute | solution.py:261
  53.3 30.0 %collective-permute-start.13 = (bf16[256,768]{1,0:T(8,128)(2,1)S(1)}, bf16[256,768]{1,0:T(8,128)(2,1)S(1)}, u32[]{:S(2)}, u32[]{:S(2)}) collective-permute-start(bf16[256,768]{1,0:T(8,128)(2,1)S(1)} %get-tuple-element.53), channel_id=1, source_target_pairs={{0,88},{8,64},{16,72},{24,80},{32,120},{40,96},{48,104},{56,112},{... | collective-permute-start | bytes 1179656 | tf_op jit(solution)/shard_map/ppermute | solution.py:261
  68.8 17.7 %collective-permute-start.14 = (bf16[256,768]{1,0:T(8,128)(2,1)S(1)}, bf16[256,768]{1,0:T(8,128)(2,1)S(1)}, u32[]{:S(2)}, u32[]{:S(2)}) collective-permute-start(bf16[256,768]{1,0:T(8,128)(2,1)S(1)} %get-tuple-element.54), channel_id=1, source_target_pairs={{0,8},{8,16},{16,24},{24,0},{32,40},{40,48},{48,56},{56,32},{64,72... | collective-permute-start | bytes 1179656 | tf_op jit(solution)/shard_map/ppermute | solution.py:261
  78.9 15.0 %collective-permute-start.9 = (bf16[256,768]{1,0:T(8,128)(2,1)S(1)}, bf16[256,768]{1,0:T(8,128)(2,1)S(1)}, u32[]{:S(2)}, u32[]{:S(2)}) collective-permute-start(bf16[256,768]{1,0:T(8,128)(2,1)S(1)} %get-tuple-element.48), channel_id=1, source_target_pairs={{0,96},{8,104},{16,112},{24,120},{32,0},{40,8},{48,16},{56,24},{64... | collective-permute-start | bytes 1179656 | tf_op jit(solution)/shard_map/ppermute | solution.py:261
  79.0 20.2 %collective-permute-start.10 = (bf16[256,768]{1,0:T(8,128)(2,1)S(1)}, bf16[256,768]{1,0:T(8,128)(2,1)S(1)}, u32[]{:S(2)}, u32[]{:S(2)}) collective-permute-start(bf16[256,768]{1,0:T(8,128)(2,1)S(1)} %get-tuple-element.50), channel_id=1, source_target_pairs={{0,112},{8,120},{16,96},{24,104},{32,16},{40,24},{48,0},{56,8},{64... | collective-permute-start | bytes 1179656 | tf_op jit(solution)/shard_map/ppermute | solution.py:261
  83.3 21.1 %collective-permute-start.6 = (bf16[256,768]{1,0:T(8,128)(2,1)S(1)}, bf16[256,768]{1,0:T(8,128)(2,1)S(1)}, u32[]{:S(2)}, u32[]{:S(2)}) collective-permute-start(bf16[256,768]{1,0:T(8,128)(2,1)S(1)} %get-tuple-element.43), channel_id=1, source_target_pairs={{0,32},{8,40},{16,48},{24,56},{32,64},{40,72},{48,80},{56,88},{64,... | collective-permute-start | bytes 1179656 | tf_op jit(solution)/shard_map/ppermute | solution.py:261
  86.5 20.1 %collective-permute-start.7 = (bf16[256,768]{1,0:T(8,128)(2,1)S(1)}, bf16[256,768]{1,0:T(8,128)(2,1)S(1)}, u32[]{:S(2)}, u32[]{:S(2)}) collective-permute-start(bf16[256,768]{1,0:T(8,128)(2,1)S(1)} %get-tuple-element.45), channel_id=1, source_target_pairs={{0,80},{8,88},{16,64},{24,72},{32,112},{40,120},{48,96},{56,104},{... | collective-permute-start | bytes 1179656 | tf_op jit(solution)/shard_map/ppermute | solution.py:261
  111.0 1.3 collective-permute-start.15
  112.2 12.3 %collective-permute-start.18 = (f32[2048]{0:T(1024)S(1)}, f32[2048]{0:T(1024)S(1)}, u32[]{:S(2)}, u32[]{:S(2)}) collective-permute-start(f32[2048]{0:T(1024)S(1)} %add.409), channel_id=1, source_target_pairs={{0,6},{1,7},{2,4},{3,5},{4,2},{5,3},{6,0},{7,1},{8,14},{9,15},{10,... | collective-permute-start | bytes 24584 | tf_op jit(solution)/shard_map/ppermute | solution.py:269
  122.9 5.2 %collective-permute-start.17 = (f32[2048]{0:T(1024)S(1)}, f32[2048]{0:T(1024)S(1)}, u32[]{:S(2)}, u32[]{:S(2)}) collective-permute-start(f32[2048]{0:T(1024)S(1)} %add.409), channel_id=1, source_target_pairs={{0,4},{1,5},{2,6},{3,7},{4,0},{5,1},{6,2},{7,3},{8,12},{9,13},{10,... | collective-permute-start | bytes 24584 | tf_op jit(solution)/shard_map/ppermute | solution.py:269
  124.2 3.9 %collective-permute-start.16 = (f32[2048]{0:T(1024)S(1)}, f32[2048]{0:T(1024)S(1)}, u32[]{:S(2)}, u32[]{:S(2)}) collective-permute-start(f32[2048]{0:T(1024)S(1)} %add.409), channel_id=1, source_target_pairs={{0,2},{1,3},{2,0},{3,1},{4,6},{5,7},{6,4},{7,5},{8,10},{9,11},{10,... | collective-permute-start | bytes 24584 | tf_op jit(solution)/shard_map/ppermute | solution.py:269

commit v4 on v3

--- a/solution.py
+++ b/solution.py
@@ -12,11 +12,12 @@
 LANES = 128
 CALL_LIMIT = 32
 HEAD = 5
-ORDER = (
-    (1, 1), (3, 3), (1, 3), (3, 1), (2, 0), (0, 2), (2, 1), (0, 3),
-    (2, 3), (0, 1), (1, 2), (3, 0), (3, 2), (1, 0), (2, 2),
+PAIRED = (
+    ((1, 1), (3, 3)), ((3, 3), (1, 1)), ((1, 3), (3, 1)), ((3, 1), (1, 3)), ((2, 0), (0, 2)),
+    ((0, 2), (2, 0)), ((2, 1), (0, 3)), ((0, 3), (2, 1)), ((2, 3), (0, 1)), ((0, 1), (2, 3)),
+    ((1, 2), (3, 0)), ((3, 0), (1, 2)), ((3, 2), (1, 0)), ((1, 0), (3, 2)), ((2, 2), (2, 2)),
 )
-CALLS = ((0, 7, 8, 11), (7, 11, 8, 15), (11, 14, 8, 15), (14, 16, 4, 15))
+CALLS = ((0, 7, 8, 11), (7, 11, 8, 15), (11, 15, 8, 15), (15, 16, 4, 15))
 
 
 def inverse_norm(values):
@@ -115,11 +116,11 @@
         sums[qb : qb + 1, :] = jnp.sum(acc[qb].T, axis=0, keepdims=True)
 
 
-def take_kernel(codes, wanted, to, candidates, *refs):
+def take_kernel(places, wanted, to, candidates, *refs):
     outs, sem = refs[:-1], refs[-1]
     copies = []
-    for i, code in enumerate(codes):
-        start = pl.multiple_of(wanted[to[code]] * BLK, BLK)
+    for i, place in enumerate(places):
+        start = pl.multiple_of(wanted[to[place]] * BLK, BLK)
         copies.append(
             pltpu.make_async_copy(candidates.at[pl.ds(start, BLK)], outs[i], sem.at[i])
         )
@@ -129,23 +130,21 @@
         copy.wait()
 
 
-def take_blocks(offsets, wanted, to, candidates):
-    side = math.isqrt(to.shape[0])
+def take_blocks(places, wanted, to, candidates):
     smem = pl.BlockSpec(memory_space=pltpu.SMEM)
     hbm = pl.BlockSpec(memory_space=pl.ANY)
-    codes = tuple(dy * side + dz for dy, dz in offsets)
     return list(
         pl.pallas_call(
-            functools.partial(take_kernel, codes),
+            functools.partial(take_kernel, tuple(places)),
             out_shape=(
                 jax.ShapeDtypeStruct((BLK, candidates.shape[1]), candidates.dtype),
             )
-            * len(codes),
+            * len(places),
             in_specs=[smem, smem, pl.BlockSpec(memory_space=pltpu.HBM)],
-            out_specs=(hbm,) * len(codes),
-            scratch_shapes=[pltpu.SemaphoreType.DMA((len(codes),))],
+            out_specs=(hbm,) * len(places),
+            scratch_shapes=[pltpu.SemaphoreType.DMA((len(places),))],
             compiler_params=pltpu.CompilerParams(vmem_limit_bytes=1 << 20),
-            name="take_%d" % len(codes),
+            name="take_%d" % len(places),
         )(wanted, to, pltpu.with_memory_space_constraint(candidates, pltpu.HBM))
     )
 
@@ -196,18 +195,20 @@
     my_y, my_z = me // side, me % side
     wanted = lax.all_to_all(requests, "rows", split_axis=0, concat_axis=0, tiled=True)[:, 0]
 
-    offsets = ((0, 0),) + ORDER
-    key_of = [0] * row_count
-    for call, (lo, hi, _, _) in enumerate(CALLS):
-        for rank in range(lo, hi):
-            dy, dz = offsets[rank]
-            key_of[dy * side + dz] = (call * row_count + rank - lo) * 8
+    odd = lax.axis_index("cols") % 2
+    keys_of = []
+    for parity in range(2):
+        keys_of.append([0] * row_count)
+        for call, (lo, hi, _, _) in enumerate(CALLS):
+            for rank in range(lo, hi):
+                dy, dz = PAIRED[rank - 1][parity] if rank else (0, 0)
+                keys_of[parity][dy * side + dz] = (call * row_count + rank - lo) * 8
     slots = pairs[:, 1]
     away = ((my_y - slots // side) % side) * side + (my_z - slots % side) % side
     ids = jnp.arange(pair_count, dtype=jnp.int32)
     key = pairs[:, 0]
-    for code, value in enumerate(key_of):
-        key = key + jnp.where(away == code, value, 0)
+    for code, values in enumerate(zip(*keys_of)):
+        key = key + jnp.where(away == code, jnp.where(odd == 1, values[1], values[0]), 0)
     key = jnp.where(ids < counts[0], key, CALL_LIMIT * row_count * 8)
     less = key[None, :] < key[:, None]
     twin = (key[None, :] == key[:, None]) & (ids[None, :] < ids[:, None])
@@ -225,9 +226,13 @@
     starts = jnp.where(wide == CALL_LIMIT, counts[0], starts)
     meta = jnp.stack([sorted_ids, tile_key, first_pair, starts])
 
-    codes = jnp.arange(row_count, dtype=jnp.int32)
-    to = ((my_y + codes // side) % side) * side + (my_z + codes % side) % side
-    sends = take_blocks(ORDER[:HEAD], wanted, to, candidates)
+    along = [
+        [jnp.array([step[parity][axis] for step in PAIRED] + [0], jnp.int32) for axis in (0, 1)]
+        for parity in (0, 1)
+    ]
+    dys, dzs = (jnp.where(odd == 1, along[1][axis], along[0][axis]) for axis in (0, 1))
+    to = ((my_y + dys) % side) * side + (my_z + dzs) % side
+    sends = take_blocks(range(HEAD), wanted, to, candidates)
     arrived = [None]
     out, sums, scored = None, [], 0
 
@@ -240,10 +245,10 @@
         sums.append(part)
         return out
 
-    for k, (dy, dz) in enumerate(ORDER):
+    for k, step in enumerate(PAIRED):
         if k == HEAD:
             to = lax.optimization_barrier((to, arrived[1]))[0]
-            sends += take_blocks(ORDER[HEAD:] + ((0, 0),), wanted, to, candidates)
+            sends += take_blocks(range(HEAD, row_count), wanted, to, candidates)
             arrived[0] = sends.pop()
             inv_q = inverse_norm(lax.optimization_barrier((queries, arrived[1]))[0])
             inv_q = jnp.broadcast_to(inv_q[:, None], (queries.shape[0], LANES))
@@ -253,12 +258,14 @@
             scored += 1
         if sums:
             send = lax.optimization_barrier((send, sums[-1]))[0]
-        perm = [
-            (y * side + z, ((y + dy) % side) * side + (z + dz) % side)
-            for y in range(side)
-            for z in range(side)
-        ]
-        arrived.append(lax.ppermute(send, "rows", perm))
+        perm = []
+        for y in range(side):
+            for z in range(side):
+                for col in range(col_count):
+                    dy, dz = step[col % 2]
+                    target = ((y + dy) % side) * side + (z + dz) % side
+                    perm.append(((y * side + z) * col_count + col, target * col_count + col))
+        arrived.append(lax.ppermute(send, ("rows", "cols"), perm))
     while scored < len(CALLS):
         out = score(out, scored)
         scored += 1

time: 129 us -> 125 us (0.969); the launches traced: 129 us -> 123 us
  starting transfers between devices: 58.1 us -> 42.4 us
  waiting for transfers between devices: 32.1 us -> 38.1 us
  Pallas kernels: 31.3 us -> 34.7 us
    ppermute x15, starting transfers between devices: 37.7 us -> 28 us  [per_device(): arrived.append(lax.ppermute(send, ('rows', 'cols'), perm))]
    ppermute x15, waiting for transfers between devices: 23.8 us -> 30.2 us  [per_device(): arrived.append(lax.ppermute(send, ('rows', 'cols'), perm))]
    ppermute x4, starting transfers between devices: 12 us -> 6.02 us  [other(): lax.ppermute(values, 'cols', [(i, i ^ flip) for i in range(col_count)])]
    pallas_call x4, Pallas kernels: 26.3 us -> 29.5 us  [score_pairs(): pl.pallas_call(functools.partial(pair_kernel, call, n_src, unroll, zero_f...]
  transfers between devices with their start and end apart: 20 -> 20, of which waited for: 9 -> 7; matrix products, arithmetic and copies ran while one was open for 3% -> 3% of each run, Pallas kernels for 19% -> 23%
where the time goes in v4:
time: 125 us; the launch traced here: 123 us
  starting transfers between devices  42.4 us (34%)
  waiting for transfers between devices  38.1 us (30%)
  Pallas kernels  34.7 us (28%)
  other arithmetic  4.64 us (4%)
  local copies, waits for them, and re-layouts  1.81 us (1%)
  between operations  1.52 us (1%)
    ppermute x15, waiting for transfers between devices, per_device(): arrived.append(lax.ppermute(send, ('rows', 'cols'), perm))  30.2 us
    pallas_call x4, Pallas kernels, score_pairs(): pl.pallas_call(functools.partial(pair_kernel, call, n_src, unroll, zero_f...  29.5 us
    ppermute x15, starting transfers between devices, per_device(): arrived.append(lax.ppermute(send, ('rows', 'cols'), perm))  28 us
    all_to_all x1, starting transfers between devices, per_device(): lax.all_to_all(requests, 'rows', split_axis=0, concat_axis=0, tiled=True)  8.41 us
    ppermute x4, starting transfers between devices, other(): lax.ppermute(values, 'cols', [(i, i ^ flip) for i in range(col_count)])  6.02 us
    ppermute x4, waiting for transfers between devices, other(): lax.ppermute(values, 'cols', [(i, i ^ flip) for i in range(col_count)])  5.42 us
    pallas_call x2, Pallas kernels, take_blocks(): pl.pallas_call(functools.partial(take_kernel, tuple(places)), out_shape=(...  5.14 us
  transfers between devices with their start and end apart: 20, of which 7 were waited for; matrix products, arithmetic and copies ran while one was open for 3% of the time, Pallas kernels for 23%

profile of v4, /device:TPU:8, one launch (start us, length us, event | category | flops | bytes accessed | tf_op | source)
XLA Modules:
  0.0 123.2 jit_solution(15540791076491030709)
XLA Ops:
  0.6 1.5 %copy.16 = s32[16,1,1]{2,1,0:T(1,128)} copy(s32[16,1,1]{0,2,1:T(1,128)} %bitcast.37) | data formatting | bytes 128 | tf_op jit(solution)/shard_map/all_to_all | solution.py:196
  2.1 8.4 %all-to-all-start = ((s32[16,1,1]{2,1,0:T(1,128)}), s32[16,1,1]{2,1,0:T(1,128)S(1)}, u32[]{:S(2)}, u32[]{:S(2)}) async-start(s32[16,1,1]{2,1,0:T(1,128)} %copy.16), calls=%async_computation | async-start | bytes 16384 | tf_op jit(solution)/shard_map/all_to_all | solution.py:196
  11.2 0.8 fusion.25
  12.0 0.8 and_select_fusion.2
  13.2 0.7 fusion.5.to
  14.2 2.5 %all-to-all-done = s32[16,1,1]{2,1,0:T(1,128)S(1)} async-done(((s32[16,1,1]{2,1,0:T(1,128)}), s32[16,1,1]{2,1,0:T(1,128)S(1)}, u32[]{:S(2)}, u32[]{:S(2)}) %all-to-all-start) | async-done | bytes 96 | tf_op jit(solution)/shard_map/all_to_all | solution.py:196
  17.0 2.1 %take_5.1 = (bf16[256,768]{1,0:T(8,128)(2,1)S(1)}, bf16[256,768]{1,0:T(8,128)(2,1)S(1)}, bf16[256,768]{1,0:T(8,128)(2,1)S(1)}, bf16[256,768]{1,0:T(8,128)(2,1)S(1)}, bf16[256,768]{1,0:T(8,128)(2,1)S(1)}) custom-call(s32[16]{0:T(128)S(1)} %reduce.wanted, s32[16]{0:T(128)S(1)} %fusion.5.to, bf16[2048,768]{1,0:T(8,128)(2,1)} %candidates.3), custom_call_target="tpu_custom_call" | custom-call | tf_op jit(solution)/shard_map/take_5/pallas_call | solution.py:137
  19.1 0.6 collective-permute-start
  19.8 3.7 %collective-permute-start.1 = (bf16[256,768]{1,0:T(8,128)(2,1)S(1)}, bf16[256,768]{1,0:T(8,128)(2,1)S(1)}, u32[]{:S(2)}, u32[]{:S(2)}) collective-permute-start(bf16[256,768]{1,0:T(8,128)(2,1)S(1)} %get-tuple-element.37), channel_id=1, source_target_pairs={{0,120},{1,41},{2,122},{3,43},{4,124},{5,45},{6,126},{7,47},{8,96}... | collective-permute-start | bytes 1179656 | tf_op jit(solution)/shard_map/ppermute | solution.py:268
  23.5 2.9 %collective-permute-start.3 = (bf16[256,768]{1,0:T(8,128)(2,1)S(1)}, bf16[256,768]{1,0:T(8,128)(2,1)S(1)}, u32[]{:S(2)}, u32[]{:S(2)}) collective-permute-start(bf16[256,768]{1,0:T(8,128)(2,1)S(1)} %get-tuple-element.39), channel_id=1, source_target_pairs={{0,104},{1,57},{2,106},{3,59},{4,108},{5,61},{6,110},{7,63},{8,112... | collective-permute-start | bytes 1179656 | tf_op jit(solution)/shard_map/ppermute | solution.py:268
  26.4 1.4 %collective-permute-start.4 = (bf16[256,768]{1,0:T(8,128)(2,1)S(1)}, bf16[256,768]{1,0:T(8,128)(2,1)S(1)}, u32[]{:S(2)}, u32[]{:S(2)}) collective-permute-start(bf16[256,768]{1,0:T(8,128)(2,1)S(1)} %get-tuple-element.40), channel_id=1, source_target_pairs={{0,64},{1,17},{2,66},{3,19},{4,68},{5,21},{6,70},{7,23},{8,72},{9,... | collective-permute-start | bytes 1179656 | tf_op jit(solution)/shard_map/ppermute | solution.py:268
  27.8 11.8 %collective-permute-done.refs_1_ = bf16[256,768]{1,0:T(8,128)(2,1)S(1)} collective-permute-done((bf16[256,768]{1,0:T(8,128)(2,1)S(1)}, bf16[256,768]{1,0:T(8,128)(2,1)S(1)}, u32[]{:S(2)}, u32[]{:S(2)}) %collective-permute-start) | collective-permute-done | bytes 393248 | tf_op jit(solution)/shard_map/ppermute | solution.py:268
  39.6 3.0 %take_11.1 = (bf16[256,768]{1,0:T(8,128)(2,1)S(1)}, bf16[256,768]{1,0:T(8,128)(2,1)S(1)}, bf16[256,768]{1,0:T(8,128)(2,1)S(1)}, bf16[256,768]{1,0:T(8,128)(2,1)S...) custom-call(s32[16]{0:T(128)S(1)} %reduce.wanted, ...), custom_call_target="tpu_custom_call" | custom-call | tf_op jit(solution)/shard_map/take_11/pallas_call | solution.py:137
  42.7 0.7 multiply_reduce_fusion
  43.4 2.4 %collective-permute-start.7 = (bf16[256,768]{1,0:T(8,128)(2,1)S(1)}, bf16[256,768]{1,0:T(8,128)(2,1)S(1)}, u32[]{:S(2)}, u32[]{:S(2)}) collective-permute-start(bf16[256,768]{1,0:T(8,128)(2,1)S(1)} %get-tuple-element.44), channel_id=1, source_target_pairs={{0,48},{1,97},{2,50},{3,99},{4,52},{5,101},{6,54},{7,103},{8,56},{... | collective-permute-start | bytes 1179656 | tf_op jit(solution)/shard_map/ppermute | solution.py:268
  45.8 1.3 %collective-permute-start.11 = (bf16[256,768]{1,0:T(8,128)(2,1)S(1)}, bf16[256,768]{1,0:T(8,128)(2,1)S(1)}, u32[]{:S(2)}, u32[]{:S(2)}) collective-permute-start(bf16[256,768]{1,0:T(8,128)(2,1)S(1)} %get-tuple-element.51), channel_id=1, source_target_pairs={{0,72},{1,25},{2,74},{3,27},{4,76},{5,29},{6,78},{7,31},{8,80},{9,... | collective-permute-start | bytes 1179656 | tf_op jit(solution)/shard_map/ppermute | solution.py:268
  47.1 5.5 %collective-permute-start.12 = (bf16[256,768]{1,0:T(8,128)(2,1)S(1)}, bf16[256,768]{1,0:T(8,128)(2,1)S(1)}, u32[]{:S(2)}, u32[]{:S(2)}) collective-permute-start(bf16[256,768]{1,0:T(8,128)(2,1)S(1)} %get-tuple-element.52), channel_id=1, source_target_pairs={{0,24},{1,73},{2,26},{3,75},{4,28},{5,77},{6,30},{7,79},{8,0},{9,8... | collective-permute-start | bytes 1179656 | tf_op jit(solution)/shard_map/ppermute | solution.py:268
  52.6 4.1 %collective-permute-start.13 = (bf16[256,768]{1,0:T(8,128)(2,1)S(1)}, bf16[256,768]{1,0:T(8,128)(2,1)S(1)}, u32[]{:S(2)}, u32[]{:S(2)}) collective-permute-start(bf16[256,768]{1,0:T(8,128)(2,1)S(1)} %get-tuple-element.53), channel_id=1, source_target_pairs={{0,88},{1,9},{2,90},{3,11},{4,92},{5,13},{6,94},{7,15},{8,64},{9,1... | collective-permute-start | bytes 1179656 | tf_op jit(solution)/shard_map/ppermute | solution.py:268
  56.7 9.3 %collective-permute-done.5.refs_6_ = bf16[256,768]{1,0:T(8,128)(2,1)S(1)} collective-permute-done((bf16[256,768]{1,0:T(8,128)(2,1)S(1)}, bf16[256,768]{1,0:T(8,128)(2,1)S(1)}, u32[]{:S(2)}, u32[]{:S(2)}) %collective-permute-start.5) | collective-permute-done | bytes 393248 | tf_op jit(solution)/shard_map/ppermute | solution.py:268
  66.3 12.0 %pairs_0.1 = (bf16[128,256,256]{2,1,0:T(8,128)(2,1)}, f32[8,256]{1,0:T(8,128)S(1)}) custom-call(s32[4,256]{1,0:T(4,128)S(1)} %pad_add_fusion.meta, bf16[2048,768]{1,0:T(8,128)(2,1)S(1)} %copy-done, f32[2048,128]{1,0:T(8,128)S(1)} %broadcast_in_dim.189.iq, bf16[256,768]{1,0:T(8,128)(2,1)S(1)} %get-tuple-element.36.refs_0_, ...), custom_call_target="tpu_custom_call" | custom-call | flops 5637144576 | bytes 7340032 | tf_op jit(solution)/shard_map/pairs_0/pallas_call | solution.py:159
  78.4 0.6 collective-permute-start.9
  79.1 1.9 %collective-permute-start.10 = (bf16[256,768]{1,0:T(8,128)(2,1)S(1)}, bf16[256,768]{1,0:T(8,128)(2,1)S(1)}, u32[]{:S(2)}, u32[]{:S(2)}) collective-permute-start(bf16[256,768]{1,0:T(8,128)(2,1)S(1)} %get-tuple-element.50), channel_id=1, source_target_pairs={{0,32},{1,113},{2,34},{3,115},{4,36},{5,117},{6,38},{7,119},{8,40}... | collective-permute-start | bytes 1179656 | tf_op jit(solution)/shard_map/ppermute | solution.py:268
  81.0 3.4 %collective-permute-start.6 = (bf16[256,768]{1,0:T(8,128)(2,1)S(1)}, bf16[256,768]{1,0:T(8,128)(2,1)S(1)}, u32[]{:S(2)}, u32[]{:S(2)}) collective-permute-start(bf16[256,768]{1,0:T(8,128)(2,1)S(1)} %get-tuple-element.43), channel_id=1, source_target_pairs={{0,80},{1,81},{2,82},{3,83},{4,84},{5,85},{6,86},{7,87},{8,88},{9,... | collective-permute-start | bytes 1179656 | tf_op jit(solution)/shard_map/ppermute | solution.py:268
  84.4 7.0 %pairs_1.1 = (bf16[128,256,256]{2,1,0:T(8,128)(2,1)}, f32[8,256]{1,0:T(8,128)S(1)}) custom-call(s32[4,256]{1,0:T(4,128)S(1)} %pad_add_fusion.meta, bf16[2048,768]{1,0:T(8,128)(2,1)S(1)} %copy-done, f32[2048,128]{1,0:T(8,128)S(1)} %broadcast_in_dim.189.iq, bf16[256,768]{1,0:T(8,128)(2,1)S(1)} %collective-permute-done.11.refs_0_, ...), custom_call_target="tpu_custom_call", output_to_operand_aliasing={{0}: (7, {})} | custom-call | flops 3221225472 | bytes 4194304 | tf_op jit(solution)/shard_map/pairs_1/pallas_call | solution.py:159
  91.5 9.1 %collective-permute-done.9.refs_2_ = bf16[256,768]{1,0:T(8,128)(2,1)S(1)} collective-permute-done((bf16[256,768]{1,0:T(8,128)(2,1)S(1)}, bf16[256,768]{1,0:T(8,128)(2,1)S(1)}, u32[]{:S(2)}, u32[]{:S(2)}) %collective-permute-start.9) | collective-permute-done | bytes 393248 | tf_op jit(solution)/shard_map/ppermute | solution.py:268
  100.6 5.8 %pairs_2.1 = (bf16[128,256,256]{2,1,0:T(8,128)(2,1)}, f32[8,256]{1,0:T(8,128)S(1)}) custom-call(s32[4,256]{1,0:T(4,128)S(1)} %pad_add_fusion.meta, bf16[2048,768]{1,0:T(8,128)(2,1)S(1)} %copy-done, f32[2048,128]{1,0:T(8,128)S(1)} %broadcast_in_dim.189.iq, bf16[256,768]{1,0:T(8,128)(2,1)S(1)} %collective-permute-done.7.refs_0_, ...), custom_call_target="tpu_custom_call", output_to_operand_aliasing={{0}: (7, {})} | custom-call | flops 3221225472 | bytes 4194304 | tf_op jit(solution)/shard_map/pairs_2/pallas_call | solution.py:159
  106.4 4.7 %pairs_3.1 = (bf16[128,256,256]{2,1,0:T(8,128)(2,1)}, f32[8,256]{1,0:T(8,128)S(1)}) custom-call(s32[4,256]{1,0:T(4,128)S(1)} %pad_add_fusion.meta, bf16[2048,768]{1,0:T(8,128)(2,1)S(1)} %copy-done, f32[2048,128]{1,0:T(8,128)S(1)} %broadcast_in_dim.189.iq, bf16[256,768]{1,0:T(8,128)(2,1)S(1)} %collective-permute-done.6.refs_0_, ...), custom_call_target="tpu_custom_call", output_to_operand_aliasing={{0}: (4, {})} | custom-call | flops 805306368 | bytes 1048576 | tf_op jit(solution)/shard_map/pairs_3/pallas_call | solution.py:159
  111.2 1.2 collective-permute-done.15
  112.4 5.0 %collective-permute-start.18 = (f32[2048]{0:T(1024)S(1)}, f32[2048]{0:T(1024)S(1)}, u32[]{:S(2)}, u32[]{:S(2)}) collective-permute-start(f32[2048]{0:T(1024)S(1)} %add.410), channel_id=1, source_target_pairs={{0,6},{1,7},{2,4},{3,5},{4,2},{5,3},{6,0},{7,1},{8,14},{9,15},{10,... | collective-permute-start | bytes 24584 | tf_op jit(solution)/shard_map/ppermute | solution.py:276
  117.4 0.9 collective-permute-start.17
  118.3 0.7 collective-permute-done.18
  119.1 3.5 %collective-permute-done.17 = f32[2048]{0:T(1024)S(1)} collective-permute-done((f32[2048]{0:T(1024)S(1)}, f32[2048]{0:T(1024)S(1)}, u32[]{:S(2)}, u32[]{:S(2)}) %collective-permute-start.17) | collective-permute-done | bytes 8224 | tf_op jit(solution)/shard_map/ppermute | solution.py:276
  (37 shorter events, 2.3 us)
Async XLA Ops:
  0.6 42.1 %copy-start = (bf16[2048,768]{1,0:T(8,128)(2,1)S(1)}, bf16[2048,768]{1,0:T(8,128)(2,1)}, u32[]{:S(2)}) copy-start(bf16[2048,768]{1,0:T(8,128)(2,1)} %q.7) | copy-start | bytes 9437188
  2.1 14.5 %all-to-all-start = ((s32[16,1,1]{2,1,0:T(1,128)}), s32[16,1,1]{2,1,0:T(1,128)S(1)}, u32[]{:S(2)}, u32[]{:S(2)}) async-start(s32[16,1,1]{2,1,0:T(1,128)} %copy.16), calls=%async_computation | async-start | bytes 16384 | tf_op jit(solution)/shard_map/all_to_all | solution.py:196
  19.1 20.4 %collective-permute-start = (bf16[256,768]{1,0:T(8,128)(2,1)S(1)}, bf16[256,768]{1,0:T(8,128)(2,1)S(1)}, u32[]{:S(2)}, u32[]{:S(2)}) collective-permute-start(bf16[256,768]{1,0:T(8,128)(2,1)S(1)} %get-tuple-element.32), channel_id=1, source_target_pairs={{0,40},{1,121},{2,42},{3,123},{4,44},{5,125},{6,46},{7,127},{8,48}... | collective-permute-start | bytes 1179656 | tf_op jit(solution)/shard_map/ppermute | solution.py:268
  19.8 23.6 %collective-permute-start.1 = (bf16[256,768]{1,0:T(8,128)(2,1)S(1)}, bf16[256,768]{1,0:T(8,128)(2,1)S(1)}, u32[]{:S(2)}, u32[]{:S(2)}) collective-permute-start(bf16[256,768]{1,0:T(8,128)(2,1)S(1)} %get-tuple-element.37), channel_id=1, source_target_pairs={{0,120},{1,41},{2,122},{3,43},{4,124},{5,45},{6,126},{7,47},{8,96}... | collective-permute-start | bytes 1179656 | tf_op jit(solution)/shard_map/ppermute | solution.py:268
  23.4 22.4 %collective-permute-start.2 = (bf16[256,768]{1,0:T(8,128)(2,1)S(1)}, bf16[256,768]{1,0:T(8,128)(2,1)S(1)}, u32[]{:S(2)}, u32[]{:S(2)}) collective-permute-start(bf16[256,768]{1,0:T(8,128)(2,1)S(1)} %get-tuple-element.38), channel_id=1, source_target_pairs={{0,56},{1,105},{2,58},{3,107},{4,60},{5,109},{6,62},{7,111},{8,32}... | collective-permute-start | bytes 1179656 | tf_op jit(solution)/shard_map/ppermute | solution.py:268
  23.5 23.7 %collective-permute-start.3 = (bf16[256,768]{1,0:T(8,128)(2,1)S(1)}, bf16[256,768]{1,0:T(8,128)(2,1)S(1)}, u32[]{:S(2)}, u32[]{:S(2)}) collective-permute-start(bf16[256,768]{1,0:T(8,128)(2,1)S(1)} %get-tuple-element.39), channel_id=1, source_target_pairs={{0,104},{1,57},{2,106},{3,59},{4,108},{5,61},{6,110},{7,63},{8,112... | collective-permute-start | bytes 1179656 | tf_op jit(solution)/shard_map/ppermute | solution.py:268
  26.4 26.2 %collective-permute-start.4 = (bf16[256,768]{1,0:T(8,128)(2,1)S(1)}, bf16[256,768]{1,0:T(8,128)(2,1)S(1)}, u32[]{:S(2)}, u32[]{:S(2)}) collective-permute-start(bf16[256,768]{1,0:T(8,128)(2,1)S(1)} %get-tuple-element.40), channel_id=1, source_target_pairs={{0,64},{1,17},{2,66},{3,19},{4,68},{5,21},{6,70},{7,23},{8,72},{9,... | collective-permute-start | bytes 1179656 | tf_op jit(solution)/shard_map/ppermute | solution.py:268
  42.6 23.4 %collective-permute-start.5 = (bf16[256,768]{1,0:T(8,128)(2,1)S(1)}, bf16[256,768]{1,0:T(8,128)(2,1)S(1)}, u32[]{:S(2)}, u32[]{:S(2)}) collective-permute-start(bf16[256,768]{1,0:T(8,128)(2,1)S(1)} %get-tuple-element.41), channel_id=1, source_target_pairs={{0,16},{1,65},{2,18},{3,67},{4,20},{5,69},{6,22},{7,71},{8,24},{9,... | collective-permute-start | bytes 1179656 | tf_op jit(solution)/shard_map/ppermute | solution.py:268
  43.4 48.0 %collective-permute-start.7 = (bf16[256,768]{1,0:T(8,128)(2,1)S(1)}, bf16[256,768]{1,0:T(8,128)(2,1)S(1)}, u32[]{:S(2)}, u32[]{:S(2)}) collective-permute-start(bf16[256,768]{1,0:T(8,128)(2,1)S(1)} %get-tuple-element.44), channel_id=1, source_target_pairs={{0,48},{1,97},{2,50},{3,99},{4,52},{5,101},{6,54},{7,103},{8,56},{... | collective-permute-start | bytes 1179656 | tf_op jit(solution)/shard_map/ppermute | solution.py:268
  45.8 32.5 %collective-permute-start.11 = (bf16[256,768]{1,0:T(8,128)(2,1)S(1)}, bf16[256,768]{1,0:T(8,128)(2,1)S(1)}, u32[]{:S(2)}, u32[]{:S(2)}) collective-permute-start(bf16[256,768]{1,0:T(8,128)(2,1)S(1)} %get-tuple-element.51), channel_id=1, source_target_pairs={{0,72},{1,25},{2,74},{3,27},{4,76},{5,29},{6,78},{7,31},{8,80},{9,... | collective-permute-start | bytes 1179656 | tf_op jit(solution)/shard_map/ppermute | solution.py:268
  47.1 31.3 %collective-permute-start.12 = (bf16[256,768]{1,0:T(8,128)(2,1)S(1)}, bf16[256,768]{1,0:T(8,128)(2,1)S(1)}, u32[]{:S(2)}, u32[]{:S(2)}) collective-permute-start(bf16[256,768]{1,0:T(8,128)(2,1)S(1)} %get-tuple-element.52), channel_id=1, source_target_pairs={{0,24},{1,73},{2,26},{3,75},{4,28},{5,77},{6,30},{7,79},{8,0},{9,8... | collective-permute-start | bytes 1179656 | tf_op jit(solution)/shard_map/ppermute | solution.py:268
  52.6 26.5 %collective-permute-start.13 = (bf16[256,768]{1,0:T(8,128)(2,1)S(1)}, bf16[256,768]{1,0:T(8,128)(2,1)S(1)}, u32[]{:S(2)}, u32[]{:S(2)}) collective-permute-start(bf16[256,768]{1,0:T(8,128)(2,1)S(1)} %get-tuple-element.53), channel_id=1, source_target_pairs={{0,88},{1,9},{2,90},{3,11},{4,92},{5,13},{6,94},{7,15},{8,64},{9,1... | collective-permute-start | bytes 1179656 | tf_op jit(solution)/shard_map/ppermute | solution.py:268
  66.0 15.0 %collective-permute-start.14 = (bf16[256,768]{1,0:T(8,128)(2,1)S(1)}, bf16[256,768]{1,0:T(8,128)(2,1)S(1)}, u32[]{:S(2)}, u32[]{:S(2)}) collective-permute-start(bf16[256,768]{1,0:T(8,128)(2,1)S(1)} %get-tuple-element.54), channel_id=1, source_target_pairs={{0,8},{1,89},{2,10},{3,91},{4,12},{5,93},{6,14},{7,95},{8,16},{9,6... | collective-permute-start | bytes 1179656 | tf_op jit(solution)/shard_map/ppermute | solution.py:268
  78.3 13.1 %collective-permute-start.8 = (bf16[256,768]{1,0:T(8,128)(2,1)S(1)}, bf16[256,768]{1,0:T(8,128)(2,1)S(1)}, u32[]{:S(2)}, u32[]{:S(2)}) collective-permute-start(bf16[256,768]{1,0:T(8,128)(2,1)S(1)} %get-tuple-element.46), channel_id=1, source_target_pairs={{0,96},{1,49},{2,98},{3,51},{4,100},{5,53},{6,102},{7,55},{8,104},... | collective-permute-start | bytes 1179656 | tf_op jit(solution)/shard_map/ppermute | solution.py:268
  78.4 22.1 %collective-permute-start.9 = (bf16[256,768]{1,0:T(8,128)(2,1)S(1)}, bf16[256,768]{1,0:T(8,128)(2,1)S(1)}, u32[]{:S(2)}, u32[]{:S(2)}) collective-permute-start(bf16[256,768]{1,0:T(8,128)(2,1)S(1)} %get-tuple-element.48), channel_id=1, source_target_pairs={{0,112},{1,33},{2,114},{3,35},{4,116},{5,37},{6,118},{7,39},{8,120... | collective-permute-start | bytes 1179656 | tf_op jit(solution)/shard_map/ppermute | solution.py:268
  79.1 21.5 %collective-permute-start.10 = (bf16[256,768]{1,0:T(8,128)(2,1)S(1)}, bf16[256,768]{1,0:T(8,128)(2,1)S(1)}, u32[]{:S(2)}, u32[]{:S(2)}) collective-permute-start(bf16[256,768]{1,0:T(8,128)(2,1)S(1)} %get-tuple-element.50), channel_id=1, source_target_pairs={{0,32},{1,113},{2,34},{3,115},{4,36},{5,117},{6,38},{7,119},{8,40}... | collective-permute-start | bytes 1179656 | tf_op jit(solution)/shard_map/ppermute | solution.py:268
  81.0 25.4 %collective-permute-start.6 = (bf16[256,768]{1,0:T(8,128)(2,1)S(1)}, bf16[256,768]{1,0:T(8,128)(2,1)S(1)}, u32[]{:S(2)}, u32[]{:S(2)}) collective-permute-start(bf16[256,768]{1,0:T(8,128)(2,1)S(1)} %get-tuple-element.43), channel_id=1, source_target_pairs={{0,80},{1,81},{2,82},{3,83},{4,84},{5,85},{6,86},{7,87},{8,88},{9,... | collective-permute-start | bytes 1179656 | tf_op jit(solution)/shard_map/ppermute | solution.py:268
  111.1 1.3 %collective-permute-start.15 = (f32[2048]{0:T(1024)S(1)}, f32[2048]{0:T(1024)S(1)}, u32[]{:S(2)}, u32[]{:S(2)}) collective-permute-start(f32[2048]{0:T(1024)S(1)} %bitcast.31), channel_id=1, source_target_pairs={{0,1},{1,0},{2,3},{3,2},{4,5},{5,4},{6,7},{7,6},{8,9},{9,8},{10,11... | collective-permute-start | bytes 24584 | tf_op jit(solution)/shard_map/ppermute | solution.py:276
  112.4 6.7 %collective-permute-start.18 = (f32[2048]{0:T(1024)S(1)}, f32[2048]{0:T(1024)S(1)}, u32[]{:S(2)}, u32[]{:S(2)}) collective-permute-start(f32[2048]{0:T(1024)S(1)} %add.410), channel_id=1, source_target_pairs={{0,6},{1,7},{2,4},{3,5},{4,2},{5,3},{6,0},{7,1},{8,14},{9,15},{10,... | collective-permute-start | bytes 24584 | tf_op jit(solution)/shard_map/ppermute | solution.py:276
  117.4 5.2 %collective-permute-start.17 = (f32[2048]{0:T(1024)S(1)}, f32[2048]{0:T(1024)S(1)}, u32[]{:S(2)}, u32[]{:S(2)}) collective-permute-start(f32[2048]{0:T(1024)S(1)} %add.410), channel_id=1, source_target_pairs={{0,4},{1,5},{2,6},{3,7},{4,0},{5,1},{6,2},{7,3},{8,12},{9,13},{10,... | collective-permute-start | bytes 24584 | tf_op jit(solution)/shard_map/ppermute | solution.py:276
  118.3 4.3 %collective-permute-start.16 = (f32[2048]{0:T(1024)S(1)}, f32[2048]{0:T(1024)S(1)}, u32[]{:S(2)}, u32[]{:S(2)}) collective-permute-start(f32[2048]{0:T(1024)S(1)} %add.410), channel_id=1, source_target_pairs={{0,2},{1,3},{2,0},{3,1},{4,6},{5,7},{6,4},{7,5},{8,10},{9,11},{10,... | collective-permute-start | bytes 24584 | tf_op jit(solution)/shard_map/ppermute | solution.py:276

commit v5 on v4

--- a/solution.py
+++ b/solution.py
@@ -11,7 +11,7 @@
 BLK = 256
 LANES = 128
 CALL_LIMIT = 32
-HEAD = 5
+HEAD = 6
 PAIRED = (
     ((1, 1), (3, 3)), ((3, 3), (1, 1)), ((1, 3), (3, 1)), ((3, 1), (1, 3)), ((2, 0), (0, 2)),
     ((0, 2), (2, 0)), ((2, 1), (0, 3)), ((0, 3), (2, 1)), ((2, 3), (0, 1)), ((0, 1), (2, 3)),

time: 125 us -> 122 us (0.976)
  the two profiles are of different devices: /device:TPU:8 before, /device:TPU:0 now
where the time goes in v5:
time: 122 us; the launch traced here: 123 us
  waiting for transfers between devices  40.5 us (33%)
  starting transfers between devices  40.3 us (33%)
  Pallas kernels  33.9 us (28%)
  other arithmetic  4.64 us (4%)
  local copies, waits for them, and re-layouts  1.81 us (1%)
  between operations  1.56 us (1%)
    ppermute x15, waiting for transfers between devices, per_device(): arrived.append(lax.ppermute(send, ('rows', 'cols'), perm))  31.9 us
    pallas_call x4, Pallas kernels, score_pairs(): pl.pallas_call(functools.partial(pair_kernel, call, n_src, unroll, zero_f...  28.9 us
    ppermute x15, starting transfers between devices, per_device(): arrived.append(lax.ppermute(send, ('rows', 'cols'), perm))  25.3 us
    all_to_all x1, starting transfers between devices, per_device(): lax.all_to_all(requests, 'rows', split_axis=0, concat_axis=0, tiled=True)  8.13 us
    ppermute x4, starting transfers between devices, other(): lax.ppermute(values, 'cols', [(i, i ^ flip) for i in range(col_count)])  6.85 us
    pallas_call x2, Pallas kernels, take_blocks(): pl.pallas_call(functools.partial(take_kernel, tuple(places)), out_shape=(...  4.99 us
    ppermute x4, waiting for transfers between devices, other(): lax.ppermute(values, 'cols', [(i, i ^ flip) for i in range(col_count)])  4.81 us
    all_to_all x1, waiting for transfers between devices, per_device(): lax.all_to_all(requests, 'rows', split_axis=0, concat_axis=0, tiled=True)  3.78 us
  transfers between devices with their start and end apart: 20, of which 10 were waited for; matrix products, arithmetic and copies ran while one was open for 3% of the time, Pallas kernels for 23%

profile of v5, /device:TPU:0, one launch (start us, length us, event | category | flops | bytes accessed | tf_op | source)
XLA Modules:
  0.0 122.7 jit_solution(8456174548975018409)
XLA Ops:
  0.6 1.5 %copy.16 = s32[16,1,1]{2,1,0:T(1,128)} copy(s32[16,1,1]{0,2,1:T(1,128)} %bitcast.37) | data formatting | bytes 128 | tf_op jit(solution)/shard_map/all_to_all | solution.py:196
  2.1 8.1 %all-to-all-start = ((s32[16,1,1]{2,1,0:T(1,128)}), s32[16,1,1]{2,1,0:T(1,128)S(1)}, u32[]{:S(2)}, u32[]{:S(2)}) async-start(s32[16,1,1]{2,1,0:T(1,128)} %copy.16), calls=%async_computation | async-start | bytes 16384 | tf_op jit(solution)/shard_map/all_to_all | solution.py:196
  11.0 0.8 fusion.25
  11.8 0.8 and_select_fusion.2
  13.0 0.7 fusion.5.to
  14.0 3.8 %all-to-all-done = s32[16,1,1]{2,1,0:T(1,128)S(1)} async-done(((s32[16,1,1]{2,1,0:T(1,128)}), s32[16,1,1]{2,1,0:T(1,128)S(1)}, u32[]{:S(2)}, u32[]{:S(2)}) %all-to-all-start) | async-done | bytes 96 | tf_op jit(solution)/shard_map/all_to_all | solution.py:196
  18.1 2.2 %take_6.1 = (bf16[256,768]{1,0:T(8,128)(2,1)S(1)}, bf16[256,768]{1,0:T(8,128)(2,1)S(1)}, bf16[256,768]{1,0:T(8,128)(2,1)S(1)}, bf16[256,768]{1,0:T(8,128)(2,1)S(...) custom-call(s32[16]{0:T(128)S(1)} %reduce.wanted, s32[16]{0:T(128)S(1)} %fusion.5.to, ...), custom_call_target="tpu_custom_call" | custom-call | tf_op jit(solution)/shard_map/take_6/pallas_call | solution.py:137
  20.3 0.6 collective-permute-start
  21.0 4.9 %collective-permute-start.1 = (bf16[256,768]{1,0:T(8,128)(2,1)S(1)}, bf16[256,768]{1,0:T(8,128)(2,1)S(1)}, u32[]{:S(2)}, u32[]{:S(2)}) collective-permute-start(bf16[256,768]{1,0:T(8,128)(2,1)S(1)} %get-tuple-element.37), channel_id=1, source_target_pairs={{0,120},{1,41},{2,122},{3,43},{4,124},{5,45},{6,126},{7,47},{8,96}... | collective-permute-start | bytes 1179656 | tf_op jit(solution)/shard_map/ppermute | solution.py:268
  25.8 4.1 %collective-permute-start.3 = (bf16[256,768]{1,0:T(8,128)(2,1)S(1)}, bf16[256,768]{1,0:T(8,128)(2,1)S(1)}, u32[]{:S(2)}, u32[]{:S(2)}) collective-permute-start(bf16[256,768]{1,0:T(8,128)(2,1)S(1)} %get-tuple-element.39), channel_id=1, source_target_pairs={{0,104},{1,57},{2,106},{3,59},{4,108},{5,61},{6,110},{7,63},{8,112... | collective-permute-start | bytes 1179656 | tf_op jit(solution)/shard_map/ppermute | solution.py:268
  30.0 10.7 %collective-permute-done.refs_1_ = bf16[256,768]{1,0:T(8,128)(2,1)S(1)} collective-permute-done((bf16[256,768]{1,0:T(8,128)(2,1)S(1)}, bf16[256,768]{1,0:T(8,128)(2,1)S(1)}, u32[]{:S(2)}, u32[]{:S(2)}) %collective-permute-start) | collective-permute-done | bytes 393248 | tf_op jit(solution)/shard_map/ppermute | solution.py:268
  40.6 2.8 %take_10.1 = (bf16[256,768]{1,0:T(8,128)(2,1)S(1)}, bf16[256,768]{1,0:T(8,128)(2,1)S(1)}, bf16[256,768]{1,0:T(8,128)(2,1)S(1)}, bf16[256,768]{1,0:T(8,128)(2,1)S...) custom-call(s32[16]{0:T(128)S(1)} %reduce.wanted, ...), custom_call_target="tpu_custom_call" | custom-call | tf_op jit(solution)/shard_map/take_10/pallas_call | solution.py:137
  43.5 0.7 multiply_reduce_fusion
  44.2 3.6 %collective-permute-start.7 = (bf16[256,768]{1,0:T(8,128)(2,1)S(1)}, bf16[256,768]{1,0:T(8,128)(2,1)S(1)}, u32[]{:S(2)}, u32[]{:S(2)}) collective-permute-start(bf16[256,768]{1,0:T(8,128)(2,1)S(1)} %get-tuple-element.44), channel_id=1, source_target_pairs={{0,48},{1,97},{2,50},{3,99},{4,52},{5,101},{6,54},{7,103},{8,56},{... | collective-permute-start | bytes 1179656 | tf_op jit(solution)/shard_map/ppermute | solution.py:268
  47.8 3.4 %collective-permute-start.12 = (bf16[256,768]{1,0:T(8,128)(2,1)S(1)}, bf16[256,768]{1,0:T(8,128)(2,1)S(1)}, u32[]{:S(2)}, u32[]{:S(2)}) collective-permute-start(bf16[256,768]{1,0:T(8,128)(2,1)S(1)} %get-tuple-element.52), channel_id=1, source_target_pairs={{0,24},{1,73},{2,26},{3,75},{4,28},{5,77},{6,30},{7,79},{8,0},{9,8... | collective-permute-start | bytes 1179656 | tf_op jit(solution)/shard_map/ppermute | solution.py:268
  51.2 2.7 %collective-permute-done.4.refs_5_ = bf16[256,768]{1,0:T(8,128)(2,1)S(1)} collective-permute-done((bf16[256,768]{1,0:T(8,128)(2,1)S(1)}, bf16[256,768]{1,0:T(8,128)(2,1)S(1)}, u32[]{:S(2)}, u32[]{:S(2)}) %collective-permute-start.4) | collective-permute-done | bytes 393248 | tf_op jit(solution)/shard_map/ppermute | solution.py:268
  53.9 4.4 %collective-permute-start.13 = (bf16[256,768]{1,0:T(8,128)(2,1)S(1)}, bf16[256,768]{1,0:T(8,128)(2,1)S(1)}, u32[]{:S(2)}, u32[]{:S(2)}) collective-permute-start(bf16[256,768]{1,0:T(8,128)(2,1)S(1)} %get-tuple-element.53), channel_id=1, source_target_pairs={{0,88},{1,9},{2,90},{3,11},{4,92},{5,13},{6,94},{7,15},{8,64},{9,1... | collective-permute-start | bytes 1179656 | tf_op jit(solution)/shard_map/ppermute | solution.py:268
  58.7 10.9 %pairs_0.1 = (bf16[128,256,256]{2,1,0:T(8,128)(2,1)}, f32[8,256]{1,0:T(8,128)S(1)}) custom-call(s32[4,256]{1,0:T(4,128)S(1)} %pad_add_fusion.meta, bf16[2048,768]{1,0:T(8,128)(2,1)S(1)} %copy-done, f32[2048,128]{1,0:T(8,128)S(1)} %broadcast_in_dim.189.iq, bf16[256,768]{1,0:T(8,128)(2,1)S(1)} %get-tuple-element.36.refs_0_, ...), custom_call_target="tpu_custom_call" | custom-call | flops 5637144576 | bytes 7340032 | tf_op jit(solution)/shard_map/pairs_0/pallas_call | solution.py:159
  69.5 2.1 %collective-permute-done.11.refs_0_ = bf16[256,768]{1,0:T(8,128)(2,1)S(1)} collective-permute-done((bf16[256,768]{1,0:T(8,128)(2,1)S(1)}, bf16[256,768]{1,0:T(8,128)(2,1)S(1)}, u32[]{:S(2)}, u32[]{:S(2)}) %collective-permute-start.11) | collective-permute-done | bytes 393248 | tf_op jit(solution)/shard_map/ppermute | solution.py:268
  71.7 2.0 %collective-permute-start.8 = (bf16[256,768]{1,0:T(8,128)(2,1)S(1)}, bf16[256,768]{1,0:T(8,128)(2,1)S(1)}, u32[]{:S(2)}, u32[]{:S(2)}) collective-permute-start(bf16[256,768]{1,0:T(8,128)(2,1)S(1)} %get-tuple-element.46), channel_id=1, source_target_pairs={{0,96},{1,49},{2,98},{3,51},{4,100},{5,53},{6,102},{7,55},{8,104},... | collective-permute-start | bytes 1179656 | tf_op jit(solution)/shard_map/ppermute | solution.py:268
  73.7 2.1 %collective-permute-start.9 = (bf16[256,768]{1,0:T(8,128)(2,1)S(1)}, bf16[256,768]{1,0:T(8,128)(2,1)S(1)}, u32[]{:S(2)}, u32[]{:S(2)}) collective-permute-start(bf16[256,768]{1,0:T(8,128)(2,1)S(1)} %get-tuple-element.48), channel_id=1, source_target_pairs={{0,112},{1,33},{2,114},{3,35},{4,116},{5,37},{6,118},{7,39},{8,120... | collective-permute-start | bytes 1179656 | tf_op jit(solution)/shard_map/ppermute | solution.py:268
  75.7 6.3 %collective-permute-done.13.refs_2_ = bf16[256,768]{1,0:T(8,128)(2,1)S(1)} collective-permute-done((bf16[256,768]{1,0:T(8,128)(2,1)S(1)}, bf16[256,768]{1,0:T(8,128)(2,1)S(1)}, u32[]{:S(2)}, u32[]{:S(2)}) %collective-permute-start.13) | collective-permute-done | bytes 393248 | tf_op jit(solution)/shard_map/ppermute | solution.py:268
  82.3 7.0 %pairs_1.1 = (bf16[128,256,256]{2,1,0:T(8,128)(2,1)}, f32[8,256]{1,0:T(8,128)S(1)}) custom-call(s32[4,256]{1,0:T(4,128)S(1)} %pad_add_fusion.meta, bf16[2048,768]{1,0:T(8,128)(2,1)S(1)} %copy-done, f32[2048,128]{1,0:T(8,128)S(1)} %broadcast_in_dim.189.iq, bf16[256,768]{1,0:T(8,128)(2,1)S(1)} %collective-permute-done.11.refs_0_, ...), custom_call_target="tpu_custom_call", output_to_operand_aliasing={{0}: (7, {})} | custom-call | flops 3221225472 | bytes 4194304 | tf_op jit(solution)/shard_map/pairs_1/pallas_call | solution.py:159
  89.3 6.6 %collective-permute-done.9.refs_2_ = bf16[256,768]{1,0:T(8,128)(2,1)S(1)} collective-permute-done((bf16[256,768]{1,0:T(8,128)(2,1)S(1)}, bf16[256,768]{1,0:T(8,128)(2,1)S(1)}, u32[]{:S(2)}, u32[]{:S(2)}) %collective-permute-start.9) | collective-permute-done | bytes 393248 | tf_op jit(solution)/shard_map/ppermute | solution.py:268
  95.9 3.5 %collective-permute-done.10.refs_3_ = bf16[256,768]{1,0:T(8,128)(2,1)S(1)} collective-permute-done((bf16[256,768]{1,0:T(8,128)(2,1)S(1)}, bf16[256,768]{1,0:T(8,128)(2,1)S(1)}, u32[]{:S(2)}, u32[]{:S(2)}) %collective-permute-start.10) | collective-permute-done | bytes 393248 | tf_op jit(solution)/shard_map/ppermute | solution.py:268
  99.4 7.0 %pairs_2.1 = (bf16[128,256,256]{2,1,0:T(8,128)(2,1)}, f32[8,256]{1,0:T(8,128)S(1)}) custom-call(s32[4,256]{1,0:T(4,128)S(1)} %pad_add_fusion.meta, bf16[2048,768]{1,0:T(8,128)(2,1)S(1)} %copy-done, f32[2048,128]{1,0:T(8,128)S(1)} %broadcast_in_dim.189.iq, bf16[256,768]{1,0:T(8,128)(2,1)S(1)} %collective-permute-done.7.refs_0_, ...), custom_call_target="tpu_custom_call", output_to_operand_aliasing={{0}: (7, {})} | custom-call | flops 3221225472 | bytes 4194304 | tf_op jit(solution)/shard_map/pairs_2/pallas_call | solution.py:159
  106.4 4.0 %pairs_3.1 = (bf16[128,256,256]{2,1,0:T(8,128)(2,1)}, f32[8,256]{1,0:T(8,128)S(1)}) custom-call(s32[4,256]{1,0:T(4,128)S(1)} %pad_add_fusion.meta, bf16[2048,768]{1,0:T(8,128)(2,1)S(1)} %copy-done, f32[2048,128]{1,0:T(8,128)S(1)} %broadcast_in_dim.189.iq, bf16[256,768]{1,0:T(8,128)(2,1)S(1)} %collective-permute-done.6.refs_0_, ...), custom_call_target="tpu_custom_call", output_to_operand_aliasing={{0}: (4, {})} | custom-call | flops 805306368 | bytes 1048576 | tf_op jit(solution)/shard_map/pairs_3/pallas_call | solution.py:159
  110.5 1.2 collective-permute-done.15
  111.7 4.0 %collective-permute-start.18 = (f32[2048]{0:T(1024)S(1)}, f32[2048]{0:T(1024)S(1)}, u32[]{:S(2)}, u32[]{:S(2)}) collective-permute-start(f32[2048]{0:T(1024)S(1)} %add.410), channel_id=1, source_target_pairs={{0,6},{1,7},{2,4},{3,5},{4,2},{5,3},{6,0},{7,1},{8,14},{9,15},{10,... | collective-permute-start | bytes 24584 | tf_op jit(solution)/shard_map/ppermute | solution.py:276
  115.7 2.7 %collective-permute-start.17 = (f32[2048]{0:T(1024)S(1)}, f32[2048]{0:T(1024)S(1)}, u32[]{:S(2)}, u32[]{:S(2)}) collective-permute-start(f32[2048]{0:T(1024)S(1)} %add.410), channel_id=1, source_target_pairs={{0,4},{1,5},{2,6},{3,7},{4,0},{5,1},{6,2},{7,3},{8,12},{9,13},{10,... | collective-permute-start | bytes 24584 | tf_op jit(solution)/shard_map/ppermute | solution.py:276
  118.5 2.4 %collective-permute-done.17 = f32[2048]{0:T(1024)S(1)} collective-permute-done((f32[2048]{0:T(1024)S(1)}, f32[2048]{0:T(1024)S(1)}, u32[]{:S(2)}, u32[]{:S(2)}) %collective-permute-start.17) | collective-permute-done | bytes 8224 | tf_op jit(solution)/shard_map/ppermute | solution.py:276
  120.9 1.2 %collective-permute-done.16 = f32[2048]{0:T(1024)S(1)} collective-permute-done((f32[2048]{0:T(1024)S(1)}, f32[2048]{0:T(1024)S(1)}, u32[]{:S(2)}, u32[]{:S(2)}) %collective-permute-start.16) | collective-permute-done | bytes 8224 | tf_op jit(solution)/shard_map/ppermute | solution.py:276
  (37 shorter events, 2.4 us)
Async XLA Ops:
  0.6 42.8 %copy-start = (bf16[2048,768]{1,0:T(8,128)(2,1)S(1)}, bf16[2048,768]{1,0:T(8,128)(2,1)}, u32[]{:S(2)}) copy-start(bf16[2048,768]{1,0:T(8,128)(2,1)} %q.7) | copy-start | bytes 9437188
  2.1 15.6 %all-to-all-start = ((s32[16,1,1]{2,1,0:T(1,128)}), s32[16,1,1]{2,1,0:T(1,128)S(1)}, u32[]{:S(2)}, u32[]{:S(2)}) async-start(s32[16,1,1]{2,1,0:T(1,128)} %copy.16), calls=%async_computation | async-start | bytes 16384 | tf_op jit(solution)/shard_map/all_to_all | solution.py:196
  20.3 20.3 %collective-permute-start = (bf16[256,768]{1,0:T(8,128)(2,1)S(1)}, bf16[256,768]{1,0:T(8,128)(2,1)S(1)}, u32[]{:S(2)}, u32[]{:S(2)}) collective-permute-start(bf16[256,768]{1,0:T(8,128)(2,1)S(1)} %get-tuple-element.32), channel_id=1, source_target_pairs={{0,40},{1,121},{2,42},{3,123},{4,44},{5,125},{6,46},{7,127},{8,48}... | collective-permute-start | bytes 1179656 | tf_op jit(solution)/shard_map/ppermute | solution.py:268
  21.0 23.2 %collective-permute-start.1 = (bf16[256,768]{1,0:T(8,128)(2,1)S(1)}, bf16[256,768]{1,0:T(8,128)(2,1)S(1)}, u32[]{:S(2)}, u32[]{:S(2)}) collective-permute-start(bf16[256,768]{1,0:T(8,128)(2,1)S(1)} %get-tuple-element.37), channel_id=1, source_target_pairs={{0,120},{1,41},{2,122},{3,43},{4,124},{5,45},{6,126},{7,47},{8,96}... | collective-permute-start | bytes 1179656 | tf_op jit(solution)/shard_map/ppermute | solution.py:268
  25.8 21.9 %collective-permute-start.2 = (bf16[256,768]{1,0:T(8,128)(2,1)S(1)}, bf16[256,768]{1,0:T(8,128)(2,1)S(1)}, u32[]{:S(2)}, u32[]{:S(2)}) collective-permute-start(bf16[256,768]{1,0:T(8,128)(2,1)S(1)} %get-tuple-element.38), channel_id=1, source_target_pairs={{0,56},{1,105},{2,58},{3,107},{4,60},{5,109},{6,62},{7,111},{8,32}... | collective-permute-start | bytes 1179656 | tf_op jit(solution)/shard_map/ppermute | solution.py:268
  25.8 21.9 %collective-permute-start.3 = (bf16[256,768]{1,0:T(8,128)(2,1)S(1)}, bf16[256,768]{1,0:T(8,128)(2,1)S(1)}, u32[]{:S(2)}, u32[]{:S(2)}) collective-permute-start(bf16[256,768]{1,0:T(8,128)(2,1)S(1)} %get-tuple-element.39), channel_id=1, source_target_pairs={{0,104},{1,57},{2,106},{3,59},{4,108},{5,61},{6,110},{7,63},{8,112... | collective-permute-start | bytes 1179656 | tf_op jit(solution)/shard_map/ppermute | solution.py:268
  30.0 24.0 %collective-permute-start.4 = (bf16[256,768]{1,0:T(8,128)(2,1)S(1)}, bf16[256,768]{1,0:T(8,128)(2,1)S(1)}, u32[]{:S(2)}, u32[]{:S(2)}) collective-permute-start(bf16[256,768]{1,0:T(8,128)(2,1)S(1)} %get-tuple-element.40), channel_id=1, source_target_pairs={{0,64},{1,17},{2,66},{3,19},{4,68},{5,21},{6,70},{7,23},{8,72},{9,... | collective-permute-start | bytes 1179656 | tf_op jit(solution)/shard_map/ppermute | solution.py:268
  40.6 17.7 %collective-permute-start.5 = (bf16[256,768]{1,0:T(8,128)(2,1)S(1)}, bf16[256,768]{1,0:T(8,128)(2,1)S(1)}, u32[]{:S(2)}, u32[]{:S(2)}) collective-permute-start(bf16[256,768]{1,0:T(8,128)(2,1)S(1)} %get-tuple-element.41), channel_id=1, source_target_pairs={{0,16},{1,65},{2,18},{3,67},{4,20},{5,69},{6,22},{7,71},{8,24},{9,... | collective-permute-start | bytes 1179656 | tf_op jit(solution)/shard_map/ppermute | solution.py:268
  44.2 45.1 %collective-permute-start.7 = (bf16[256,768]{1,0:T(8,128)(2,1)S(1)}, bf16[256,768]{1,0:T(8,128)(2,1)S(1)}, u32[]{:S(2)}, u32[]{:S(2)}) collective-permute-start(bf16[256,768]{1,0:T(8,128)(2,1)S(1)} %get-tuple-element.44), channel_id=1, source_target_pairs={{0,48},{1,97},{2,50},{3,99},{4,52},{5,101},{6,54},{7,103},{8,56},{... | collective-permute-start | bytes 1179656 | tf_op jit(solution)/shard_map/ppermute | solution.py:268
  47.8 23.9 %collective-permute-start.11 = (bf16[256,768]{1,0:T(8,128)(2,1)S(1)}, bf16[256,768]{1,0:T(8,128)(2,1)S(1)}, u32[]{:S(2)}, u32[]{:S(2)}) collective-permute-start(bf16[256,768]{1,0:T(8,128)(2,1)S(1)} %get-tuple-element.51), channel_id=1, source_target_pairs={{0,72},{1,25},{2,74},{3,27},{4,76},{5,29},{6,78},{7,31},{8,80},{9,... | collective-permute-start | bytes 1179656 | tf_op jit(solution)/shard_map/ppermute | solution.py:268
  47.8 25.9 %collective-permute-start.12 = (bf16[256,768]{1,0:T(8,128)(2,1)S(1)}, bf16[256,768]{1,0:T(8,128)(2,1)S(1)}, u32[]{:S(2)}, u32[]{:S(2)}) collective-permute-start(bf16[256,768]{1,0:T(8,128)(2,1)S(1)} %get-tuple-element.52), channel_id=1, source_target_pairs={{0,24},{1,73},{2,26},{3,75},{4,28},{5,77},{6,30},{7,79},{8,0},{9,8... | collective-permute-start | bytes 1179656 | tf_op jit(solution)/shard_map/ppermute | solution.py:268
  53.9 28.1 %collective-permute-start.13 = (bf16[256,768]{1,0:T(8,128)(2,1)S(1)}, bf16[256,768]{1,0:T(8,128)(2,1)S(1)}, u32[]{:S(2)}, u32[]{:S(2)}) collective-permute-start(bf16[256,768]{1,0:T(8,128)(2,1)S(1)} %get-tuple-element.53), channel_id=1, source_target_pairs={{0,88},{1,9},{2,90},{3,11},{4,92},{5,13},{6,94},{7,15},{8,64},{9,1... | collective-permute-start | bytes 1179656 | tf_op jit(solution)/shard_map/ppermute | solution.py:268
  58.3 23.7 %collective-permute-start.14 = (bf16[256,768]{1,0:T(8,128)(2,1)S(1)}, bf16[256,768]{1,0:T(8,128)(2,1)S(1)}, u32[]{:S(2)}, u32[]{:S(2)}) collective-permute-start(bf16[256,768]{1,0:T(8,128)(2,1)S(1)} %get-tuple-element.54), channel_id=1, source_target_pairs={{0,8},{1,89},{2,10},{3,91},{4,12},{5,93},{6,14},{7,95},{8,16},{9,6... | collective-permute-start | bytes 1179656 | tf_op jit(solution)/shard_map/ppermute | solution.py:268
  71.7 17.7 %collective-permute-start.8 = (bf16[256,768]{1,0:T(8,128)(2,1)S(1)}, bf16[256,768]{1,0:T(8,128)(2,1)S(1)}, u32[]{:S(2)}, u32[]{:S(2)}) collective-permute-start(bf16[256,768]{1,0:T(8,128)(2,1)S(1)} %get-tuple-element.46), channel_id=1, source_target_pairs={{0,96},{1,49},{2,98},{3,51},{4,100},{5,53},{6,102},{7,55},{8,104},... | collective-permute-start | bytes 1179656 | tf_op jit(solution)/shard_map/ppermute | solution.py:268
  73.7 22.3 %collective-permute-start.9 = (bf16[256,768]{1,0:T(8,128)(2,1)S(1)}, bf16[256,768]{1,0:T(8,128)(2,1)S(1)}, u32[]{:S(2)}, u32[]{:S(2)}) collective-permute-start(bf16[256,768]{1,0:T(8,128)(2,1)S(1)} %get-tuple-element.48), channel_id=1, source_target_pairs={{0,112},{1,33},{2,114},{3,35},{4,116},{5,37},{6,118},{7,39},{8,120... | collective-permute-start | bytes 1179656 | tf_op jit(solution)/shard_map/ppermute | solution.py:268
  82.0 17.4 %collective-permute-start.10 = (bf16[256,768]{1,0:T(8,128)(2,1)S(1)}, bf16[256,768]{1,0:T(8,128)(2,1)S(1)}, u32[]{:S(2)}, u32[]{:S(2)}) collective-permute-start(bf16[256,768]{1,0:T(8,128)(2,1)S(1)} %get-tuple-element.50), channel_id=1, source_target_pairs={{0,32},{1,113},{2,34},{3,115},{4,36},{5,117},{6,38},{7,119},{8,40}... | collective-permute-start | bytes 1179656 | tf_op jit(solution)/shard_map/ppermute | solution.py:268
  82.0 24.4 %collective-permute-start.6 = (bf16[256,768]{1,0:T(8,128)(2,1)S(1)}, bf16[256,768]{1,0:T(8,128)(2,1)S(1)}, u32[]{:S(2)}, u32[]{:S(2)}) collective-permute-start(bf16[256,768]{1,0:T(8,128)(2,1)S(1)} %get-tuple-element.43), channel_id=1, source_target_pairs={{0,80},{1,81},{2,82},{3,83},{4,84},{5,85},{6,86},{7,87},{8,88},{9,... | collective-permute-start | bytes 1179656 | tf_op jit(solution)/shard_map/ppermute | solution.py:268
  110.4 1.3 %collective-permute-start.15 = (f32[2048]{0:T(1024)S(1)}, f32[2048]{0:T(1024)S(1)}, u32[]{:S(2)}, u32[]{:S(2)}) collective-permute-start(f32[2048]{0:T(1024)S(1)} %bitcast.31), channel_id=1, source_target_pairs={{0,1},{1,0},{2,3},{3,2},{4,5},{5,4},{6,7},{7,6},{8,9},{9,8},{10,11... | collective-permute-start | bytes 24584 | tf_op jit(solution)/shard_map/ppermute | solution.py:276
  111.7 6.8 %collective-permute-start.18 = (f32[2048]{0:T(1024)S(1)}, f32[2048]{0:T(1024)S(1)}, u32[]{:S(2)}, u32[]{:S(2)}) collective-permute-start(f32[2048]{0:T(1024)S(1)} %add.410), channel_id=1, source_target_pairs={{0,6},{1,7},{2,4},{3,5},{4,2},{5,3},{6,0},{7,1},{8,14},{9,15},{10,... | collective-permute-start | bytes 24584 | tf_op jit(solution)/shard_map/ppermute | solution.py:276
  115.7 5.2 %collective-permute-start.17 = (f32[2048]{0:T(1024)S(1)}, f32[2048]{0:T(1024)S(1)}, u32[]{:S(2)}, u32[]{:S(2)}) collective-permute-start(f32[2048]{0:T(1024)S(1)} %add.410), channel_id=1, source_target_pairs={{0,4},{1,5},{2,6},{3,7},{4,0},{5,1},{6,2},{7,3},{8,12},{9,13},{10,... | collective-permute-start | bytes 24584 | tf_op jit(solution)/shard_map/ppermute | solution.py:276
  118.5 3.7 %collective-permute-start.16 = (f32[2048]{0:T(1024)S(1)}, f32[2048]{0:T(1024)S(1)}, u32[]{:S(2)}, u32[]{:S(2)}) collective-permute-start(f32[2048]{0:T(1024)S(1)} %add.410), channel_id=1, source_target_pairs={{0,2},{1,3},{2,0},{3,1},{4,6},{5,7},{6,4},{7,5},{8,10},{9,11},{10,... | collective-permute-start | bytes 24584 | tf_op jit(solution)/shard_map/ppermute | solution.py:276
